TPU v7x, 32 devices: a whole 2x2x4 slice. The times are simulated.
32 devices in a mesh: dp: 8 (over y, x, core), mp: 4 (over z).
Axes of the slice: x: 2, y: 2, z: 4, core: 2. Of those that a mesh axis runs over, the one named last changes fastest.
Arguments:
- token_ids: int32 [8, 1024], P('dp'), may hold values from 0 to 50303
- prompt_len: int32 [8], replicated, may hold values from 1 to 512, as said below
- example_len: int32 [8], replicated, may hold values from 512 to 1024, as said below
- embedding: bfloat16 [50304, 1024], P('mp'), may hold values from -6 to 6
- w_qkv: bfloat16 [1024, 3072], P(None, 'mp'), may hold values from -0.1875 to 0.1875
- w_out: bfloat16 [1024, 1024], P('mp'), may hold values from -0.75 to 0.75
- w_in: bfloat16 [1024, 4096], P(None, 'mp'), may hold values from -0.1875 to 0.1875
- b_in: float32 [4096], P('mp'), may hold values from -3 to 3
- w_down: bfloat16 [4096, 1024], P('mp'), may hold values from -0.09375 to 0.09375
- unembed: bfloat16 [1024, 50304], P('dp', 'mp'), may hold values from -0.1875 to 0.1875
- ln_gain: float32 [3, 1024], replicated, may hold values from 0.5 to 1.5
- ln_bias: float32 [3, 1024], replicated, may hold values from -3 to 3
- master: float32 [8, 1024, 128], P(None, ('dp', 'mp')), may hold values from -0.1875 to 0.1875
- first_moment: float32 [8, 1024, 128], P(None, ('dp', 'mp')), may hold values from -1.5258789e-05 to 1.5258789e-05
- second_moment: float32 [8, 1024, 128], P(None, ('dp', 'mp')), may hold values from 4.7683716e-14 to 7.6293946e-13
- eigen_bases: float32 [8, 128, 128], replicated, as said below
Outputs:
- mean_loss: float32 [], replicated
- grad_norm: float32 [], replicated
- new_first: float32 [8, 1024, 128], P(None, ('dp', 'mp'))
- new_second: float32 [8, 1024, 128], P(None, ('dp', 'mp'))
- new_master: float32 [8, 1024, 128], P(None, ('dp', 'mp'))
Inputs may be any that keep to these rules, and one draw needn't show every extreme that they name: `prompt_len`: each at most half of its example's length; the first example's is 512. `example_len`: the first example is 1024 tokens long. `eigen_bases`: each matrix is orthogonal.
All inputs are finite; a program needn't handle non-finite values.
Results may differ from a plain program's by a relative error of at most 0.0024.
Values may be sent and summed in bfloat16 or wider, within the bound.
A program may use at most 192 MiB of HBM per device.

v0:
```python
import functools

import jax
import jax.numpy as jnp
from jax import lax
from jax.experimental import pallas as pl
from jax.experimental.pallas import tpu as pltpu
from jax.sharding import PartitionSpec as P

MESH = pl.DeviceIdType.MESH
VMEM_LIMIT = 60 * 1024 * 1024

D = 1024
HEADS = 16
R = 128
ADAM_STEP = 10
HD = 64
ROT = 16


HIGH_PRECISION = lax.Precision.HIGHEST
NORM_EPS = 1e-05
ROPE_BASE = 10000.0
CLIP_LIMIT = 0.01
LEARN_RATE = 0.02
BETA_FIRST = 0.9
BETA_SECOND = 0.999
ADAM_EPS = 1e-08
DECAY_RATE = 0.01


def layer_norm(values, gain, shift):
    centre = values - jnp.mean(values, -1, keepdims=True)
    spread = jnp.mean(centre * centre, -1, keepdims=True)
    return centre * lax.rsqrt(spread + NORM_EPS) * gain + shift


def rope_tables(length):
    half = ROT // 2
    freqs = ROPE_BASE ** (-2.0 * jnp.arange(half, dtype=jnp.float32) / ROT)
    angles = jnp.arange(length, dtype=jnp.float32)[:, None] * freqs[None, :]
    return (jnp.cos(angles)[:, None, :], jnp.sin(angles)[:, None, :])


def rotate_back(upstream, cosine, sine):
    half = ROT // 2
    first = upstream[..., :half]
    second = upstream[..., half:ROT]
    return jnp.concatenate(
        [first * cosine + second * sine, second * cosine - first * sine, upstream[..., ROT:]], -1
    )


def masked_scores(queries, key_rows, start_row, stop_row):
    scores = jnp.einsum(
        "qhd,khd->hqk",
        queries[start_row:stop_row],
        key_rows[:stop_row],
        preferred_element_type=jnp.float32,
    ) * HD ** (-0.5)
    query_pos = start_row + jnp.arange(stop_row - start_row)[:, None]
    causal = jnp.arange(stop_row)[None, :] <= query_pos
    return jnp.where(causal[None], scores, -1e30)


def attend_back(queries, key_rows, value_rows, spreads, upstream):
    length = queries.shape[0]
    row_block = min(512, length)
    scaling = HD ** (-0.5)
    query_grads = []
    key_grad = jnp.zeros(key_rows.shape, jnp.float32)
    value_grad = jnp.zeros(value_rows.shape, jnp.float32)
    for start_row in range(0, length, row_block):
        stop_row = start_row + row_block
        scores = masked_scores(queries, key_rows, start_row, stop_row)
        probs = jnp.exp(scores - spreads[:, start_row:stop_row, None])
        grad_here = upstream[start_row:stop_row]
        prob_grad = jnp.einsum(
            "qhd,khd->hqk", grad_here, value_rows[:stop_row], preferred_element_type=jnp.float32
        )
        inner_sum = jnp.sum(probs * prob_grad, -1, keepdims=True)
        score_grad = (probs * (prob_grad - inner_sum)).astype(jnp.bfloat16)
        query_grads.append(
            jnp.einsum(
                "hqk,khd->qhd", score_grad, key_rows[:stop_row], preferred_element_type=jnp.float32
            )
            * scaling
        )
        key_grad = key_grad.at[:stop_row].add(
            jnp.einsum(
                "hqk,qhd->khd",
                score_grad,
                queries[start_row:stop_row],
                preferred_element_type=jnp.float32,
            )
            * scaling
        )
        value_grad = value_grad.at[:stop_row].add(
            jnp.einsum(
                "hqk,qhd->khd",
                probs.astype(jnp.bfloat16),
                grad_here,
                preferred_element_type=jnp.float32,
            )
        )
    return (jnp.concatenate(query_grads, 0), key_grad, value_grad)


def line_chunk(index, size):
    return pl.ds(pl.multiple_of(index * size, size), size)


def greet_line(me, count):
    barrier = pltpu.get_barrier_semaphore()

    @pl.when(me > 0)
    def _():
        pl.semaphore_signal(
            barrier, inc=1, device_id={"mp": jnp.maximum(me - 1, 0)}, device_id_type=MESH
        )

    @pl.when(me < count - 1)
    def _():
        pl.semaphore_signal(
            barrier, inc=1, device_id={"mp": jnp.minimum(me + 1, count - 1)}, device_id_type=MESH
        )

    peers = jnp.where(me > 0, 1, 0) + jnp.where(me < count - 1, 1, 0)
    pl.semaphore_wait(barrier, peers)


def greet_peers(me, count):
    barrier = pltpu.get_barrier_semaphore()
    for offset in range(1, count):
        pl.semaphore_signal(
            barrier, inc=1, device_id={"mp": lax.rem(me + offset, count)}, device_id_type=MESH
        )
    pl.semaphore_wait(barrier, count - 1)


def line_sum(count, chunk, own, wires, sems, prepare, emit, greet=True, follow=None, always=False):
    me = lax.axis_index("mp")
    from_low, from_high, to_high, to_low = wires
    up_send, up_recv, down_send, down_recv = sems
    length = own.shape[0]
    chunks = length // chunk
    above = jnp.minimum(me + 1, count - 1)
    below = jnp.maximum(me - 1, 0)

    def up_copy(index):
        rows = line_chunk(index, chunk)
        return pltpu.make_async_remote_copy(
            src_ref=to_high.at[rows],
            dst_ref=from_low.at[rows],
            send_sem=up_send.at[index],
            recv_sem=up_recv.at[index],
            device_id={"mp": above},
            device_id_type=MESH,
        )

    def down_copy(index):
        rows = line_chunk(index, chunk)
        return pltpu.make_async_remote_copy(
            src_ref=to_low.at[rows],
            dst_ref=from_high.at[rows],
            send_sem=down_send.at[index],
            recv_sem=down_recv.at[index],
            device_id={"mp": below},
            device_id_type=MESH,
        )

    if greet:
        greet_line(me, count)

    @pl.when(me == 0)
    def _():
        from_low[...] = jnp.zeros_like(from_low)

    @pl.when(me == count - 1)
    def _():
        from_high[...] = jnp.zeros_like(from_high)

    def step(at, carry):
        if prepare is not None and always:
            prepare(at)
        elif prepare is not None:

            @pl.when(at < chunks)
            def _():
                prepare(at)

        up = at - LINE_LAG * me

        @pl.when((up >= 0) & (up < chunks))
        def _():
            rows = line_chunk(up, chunk)

            @pl.when(me > 0)
            def _():
                up_copy(up).wait_recv()

            @pl.when(me < count - 1)
            def _():
                to_high[rows, :] = (
                    from_low[rows, :].astype(jnp.float32) + own[rows, :].astype(jnp.float32)
                ).astype(jnp.bfloat16)
                up_copy(up).start()

        down = at - LINE_LAG * (count - 1 - me)

        @pl.when((down >= 0) & (down < chunks))
        def _():
            rows = line_chunk(down, chunk)

            @pl.when(me < count - 1)
            def _():
                down_copy(down).wait_recv()

            @pl.when(me > 0)
            def _():
                to_low[rows, :] = (
                    from_high[rows, :].astype(jnp.float32) + own[rows, :].astype(jnp.float32)
                ).astype(jnp.bfloat16)
                down_copy(down).start()

        ready = at - LINE_LAG * jnp.maximum(me, count - 1 - me)

        @pl.when((ready >= 0) & (ready < chunks))
        def _():
            rows = line_chunk(ready, chunk)
            total = (
                from_low[rows, :].astype(jnp.float32)
                + own[rows, :].astype(jnp.float32)
                + from_high[rows, :].astype(jnp.float32)
            )
            emit(rows, total)
            if follow is not None:
                follow(ready)

        return carry

    lax.fori_loop(0, chunks + LINE_LAG * (count - 1), step, 0)

    def drain(index, carry):
        @pl.when(me < count - 1)
        def _():
            up_copy(index).wait_send()

        @pl.when(me > 0)
        def _():
            down_copy(index).wait_send()

        return carry

    lax.fori_loop(0, chunks, drain, 0)


PICK_GROUP = 32
PICK_ALIGN = 8


def pick_kernel(spots, places, table, out, held, sems):
    rows = out.shape[0]
    span = PICK_GROUP * PICK_ALIGN

    def start(group, carry):
        def one(token, carry):
            at = group * PICK_GROUP + token
            pltpu.make_async_copy(
                table.at[pl.ds(pl.multiple_of(spots[at], PICK_ALIGN), PICK_ALIGN)],
                held.at[pl.ds(pl.multiple_of(at * PICK_ALIGN, PICK_ALIGN), PICK_ALIGN)],
                sems.at[group],
            ).start()
            return carry

        return lax.fori_loop(0, PICK_GROUP, one, carry, unroll=8)

    lax.fori_loop(0, rows // PICK_GROUP, start, 0)

    def choose(group, carry):
        block = held.at[pl.ds(pl.multiple_of(group * span, span), span)]
        pltpu.make_async_copy(table.at[pl.ds(0, span)], block, sems.at[group]).wait()
        here = line_chunk(group, PICK_GROUP)
        wanted = places[here, :]
        column = lax.broadcasted_iota(jnp.int32, (PICK_GROUP, span), 1)
        chosen = jnp.where(column == wanted, 1.0, 0.0).astype(jnp.bfloat16)
        out[here, :] = jnp.dot(
            chosen, block[...], preferred_element_type=jnp.float32
        ).astype(jnp.bfloat16)
        return carry

    lax.fori_loop(0, rows // PICK_GROUP, choose, 0)


def pick_call(index, table, name):
    rows = index.shape[0]
    vocab, width = table.shape
    spread = (lax.iota(jnp.int32, rows) * PICK_ALIGN) % (vocab - PICK_ALIGN)
    safe = jnp.where((index >= 0) & (index < vocab), index, spread)
    spots = safe - safe % PICK_ALIGN
    column = index.reshape(rows, 1)
    token = lax.broadcasted_iota(jnp.int32, (rows, 1), 0) % PICK_GROUP
    places = jnp.where(
        (column >= 0) & (column < vocab), token * PICK_ALIGN + column % PICK_ALIGN, -1
    )
    return pl.pallas_call(
        pick_kernel,
        name=name,
        in_specs=[
            pl.BlockSpec(memory_space=pltpu.SMEM),
            pl.BlockSpec(memory_space=pltpu.VMEM),
            pl.BlockSpec(memory_space=pl.ANY),
        ],
        out_specs=pl.BlockSpec(memory_space=pltpu.VMEM),
        out_shape=jax.ShapeDtypeStruct((rows, width), jnp.bfloat16),
        scratch_shapes=[
            pltpu.VMEM((rows * PICK_ALIGN, width), jnp.bfloat16),
            pltpu.SemaphoreType.DMA((rows // PICK_GROUP,)),
        ],
        compiler_params=pltpu.CompilerParams(vmem_limit_bytes=VMEM_LIMIT),
        cost_estimate=pl.CostEstimate(
            flops=2 * rows * PICK_GROUP * PICK_ALIGN * width,
            bytes_accessed=2 * rows * PICK_ALIGN * width,
            transcendentals=0,
        ),
    )(spots, places, table)


LINE_CHUNK = 32
LINE_LAG = 3
WORK_ROWS = 256


def line_scratch(length, width):
    chunks = length // LINE_CHUNK
    return [pltpu.VMEM((length, width), jnp.bfloat16)] * 4 + [
        pltpu.SemaphoreType.DMA((chunks,))
    ] * 4


def line_call(kernel, name, collective_id, outs, scratch, operands, flops=0, spaces=()):
    size = sum(o.size * o.dtype.itemsize for o in operands) + sum(
        o.size * o.dtype.itemsize for o in outs
    )
    vmem = pl.BlockSpec(memory_space=pltpu.VMEM)
    return pl.pallas_call(
        kernel,
        name=name,
        out_shape=outs,
        in_specs=[vmem] * (len(operands) - len(spaces))
        + [pl.BlockSpec(memory_space=space) for space in spaces],
        out_specs=[vmem] * len(outs),
        scratch_shapes=scratch,
        compiler_params=pltpu.CompilerParams(
            collective_id=collective_id, has_side_effects=True, vmem_limit_bytes=VMEM_LIMIT
        ),
        cost_estimate=pl.CostEstimate(
            flops=flops, bytes_accessed=size + 100_000_000, transcendentals=0
        ),
    )(*operands)


def start_kernel(
    count,
    part,
    gain,
    shift,
    bias,
    master,
    w_qkv,
    w_in,
    w_down,
    rows_out,
    attn_out,
    base_out,
    ffn_out,
    pool_out,
    *scratch,
):
    (normed, held_qkv, turned, held_in, held_down, sems, pool, near_out, near_in, far_out, far_in) = (
        scratch[8:]
    )
    shards = pool.shape[0]
    splits = shards.bit_length() - 1
    me = lax.axis_index("dp")
    lane = lax.axis_index("mp")
    mates = [me + 2**k * (1 - 2 * ((me // 2**k) % 2)) for k in range(splits)]
    peers = [lax.rem(lane + offset, count) for offset in range(count)]
    barrier = pltpu.get_barrier_semaphore()
    for mate in mates:
        pl.semaphore_signal(barrier, inc=1, device_id={"dp": mate, "mp": lane}, device_id_type=MESH)
    for peer in peers[1:]:
        pl.semaphore_signal(barrier, inc=1, device_id={"dp": me, "mp": peer}, device_id_type=MESH)
    pl.semaphore_wait(barrier, splits + count - 1)
    pool[me, lane] = master[...].astype(jnp.bfloat16)

    def near(offset):
        return pltpu.make_async_remote_copy(
            src_ref=pool.at[me, lane],
            dst_ref=pool.at[me, lane],
            send_sem=near_out.at[offset],
            recv_sem=near_in.at[offset],
            device_id={"dp": me, "mp": peers[offset]},
            device_id_type=MESH,
        )

    def far(stage):
        bit = splits - 1 - stage
        copies = []
        for place in range(2**stage):
            slot = lax.rem(me, 2 ** (bit + 1)) + place * 2 ** (bit + 1)
            copies.append(
                pltpu.make_async_remote_copy(
                    src_ref=pool.at[slot],
                    dst_ref=pool.at[slot],
                    send_sem=far_out.at[2**stage - 1 + place],
                    recv_sem=far_in.at[2**stage - 1 + place],
                    device_id={"dp": mates[bit], "mp": lane},
                    device_id_type=MESH,
                )
            )
        return copies

    for offset in range(1, count):
        near(offset).start()

    first, last = 6, part.shape[0] // LINE_CHUNK + 2
    waits = (
        [first]
        + [
            first + (last - first) * (2 ** (stage + 1) - 1) // max(1, 2 ** (splits - 1) - 1)
            for stage in range(splits - 1)
        ]
        + [last + 6]
    )

    def prepare(at):
        for stage in range(splits + 1):

            @pl.when(at == waits[stage])
            def _(stage=stage):
                if stage == 0:
                    for offset in range(1, count):
                        near(offset).wait_recv()
                else:
                    for copy in far(stage - 1):
                        copy.wait_recv()
                if stage < splits:
                    for copy in far(stage):
                        copy.start()

    loads = [
        pltpu.make_async_copy(src, dst, sems.at[slot])
        for slot, (src, dst) in enumerate(
            ((w_qkv, held_qkv), (w_in, held_in), (w_down, held_down))
        )
    ]
    for load in loads:
        load.start()

    def emit(rows, total):
        rows_out[rows, :] = total.astype(jnp.bfloat16)
        centre = total - jnp.mean(total, -1, keepdims=True)
        spread = jnp.mean(centre * centre, -1, keepdims=True)
        base = centre * lax.rsqrt(spread + NORM_EPS)
        attn_out[rows, :] = (base * gain[0:1, :] + shift[0:1, :]).astype(jnp.bfloat16)
        normed[rows, :] = (base * gain[1:2, :] + shift[1:2, :]).astype(jnp.bfloat16)

    per = WORK_ROWS // LINE_CHUNK

    def follow(ready):
        @pl.when(ready == per - 1)
        def _():
            for load in loads:
                load.wait()
            heads = held_qkv.shape[1] // (3 * HD)
            for kind in range(3):
                for head in range(heads):
                    into = (kind * heads + head) * HD
                    source = (head * 3 + kind) * HD
                    turned[:, into : into + HD] = held_qkv[:, source : source + HD]

        @pl.when(lax.rem(ready, per) == per - 1)
        def _():
            rows = line_chunk(ready // per, WORK_ROWS)
            base_out[rows, :] = jnp.dot(
                attn_out[rows, :], turned[...], preferred_element_type=jnp.float32
            )
            pre = (
                jnp.dot(normed[rows, :], held_in[...], preferred_element_type=jnp.float32)
                + bias[...]
            )
            hidden = (0.5 * pre * (1.0 + lax.erf(pre * 0.5**0.5))).astype(jnp.bfloat16)
            ffn_out[rows, :] = jnp.dot(
                hidden, held_down[...], preferred_element_type=jnp.float32
            ).astype(jnp.bfloat16)

    line_sum(
        count,
        LINE_CHUNK,
        part,
        scratch[:4],
        scratch[4:8],
        prepare,
        emit,
        greet=False,
        follow=follow,
        always=True,
    )
    pool_out[...] = pool[...]
    for offset in range(1, count):
        near(offset).wait_send()
    for stage in range(splits):
        for copy in far(stage):
            copy.wait_send()


def turn_pairs(field, cosine, sine, sign):
    lane = lax.broadcasted_iota(jnp.int32, field.shape, 1) % HD
    half = ROT // 2
    other = jnp.where(
        lane < half, pltpu.roll(field, field.shape[1] - half, 1), pltpu.roll(field, half, 1)
    )
    return field * cosine + sign * other * sine


CROSS = (((1,), (1,)), ((), ()))


def resid_kernel(
    count,
    attn,
    base,
    ffn,
    start,
    gain,
    shift,
    cosine,
    sine,
    down_qkv,
    up_q,
    up_k,
    up_v,
    down_out,
    up_out,
    w_out,
    inner_out,
    query_out,
    key_out,
    value_out,
    context_out,
    spread_out,
    low_out,
    resid_out,
    final_out,
    *scratch,
):
    own = scratch[8]
    group = w_out.shape[0]
    total_rows = own.shape[0]
    key_out[...] = jnp.zeros_like(key_out)
    value_out[...] = jnp.zeros_like(value_out)

    def attend(block):
        rows = line_chunk(block, WORK_ROWS)
        low = jnp.dot(
            attn[rows, :], down_qkv[...], preferred_element_type=jnp.float32
        ).astype(jnp.bfloat16)
        inner_out[rows, :] = low
        for kind, (up, out) in enumerate(
            ((up_q, query_out), (up_k, key_out), (up_v, value_out))
        ):
            extra = lax.dot_general(
                low[:, kind * R : (kind + 1) * R],
                up[...],
                CROSS,
                preferred_element_type=jnp.float32,
            )
            for at in range(0, group, 128):
                field = base[rows, kind * group + at : kind * group + at + 128]
                field = field + extra[:, at : at + 128]
                if kind < 2:
                    field = turn_pairs(field, cosine[rows, :], sine[rows, :], 1.0)
                out[rows, at : at + 128] = field.astype(jnp.bfloat16)
        lane = lax.broadcasted_iota(jnp.int32, (WORK_ROWS, 128), 1)
        column = lax.broadcasted_iota(jnp.int32, (WORK_ROWS, total_rows), 1)
        place = lax.broadcasted_iota(jnp.int32, (WORK_ROWS, total_rows), 0)
        seen = column <= place + block * WORK_ROWS
        spreads = jnp.zeros((WORK_ROWS, 128), jnp.float32)
        for at in range(0, group, 128):
            pair = query_out[rows, at : at + 128]
            keys = key_out[:, at : at + 128]
            values = value_out[:, at : at + 128]
            results = []
            for side in range(128 // HD):
                mine = jnp.where(lane // HD == side, pair, jnp.zeros_like(pair))
                scores = (
                    lax.dot_general(mine, keys, CROSS, preferred_element_type=jnp.float32)
                    * HD**-0.5
                )
                scores = jnp.where(seen, scores, -1e30)
                top = jnp.max(scores, -1, keepdims=True)
                weights = jnp.exp(scores - top)
                total = jnp.sum(weights, -1, keepdims=True)
                probs = (weights * (1.0 / total)).astype(jnp.bfloat16)
                results.append(jnp.dot(probs, values, preferred_element_type=jnp.float32))
                head = at // HD + side
                spreads = jnp.where(lane == head, top + jnp.log(total), spreads)
            joined = results[0]
            for side in range(1, 128 // HD):
                joined = jnp.where(lane // HD == side, results[side], joined)
            context_out[rows, at : at + 128] = joined.astype(jnp.bfloat16)
        spread_out[rows, :] = spreads
        context = context_out[rows, :]
        low = jnp.dot(context, down_out[...], preferred_element_type=jnp.float32).astype(
            jnp.bfloat16
        )
        low_out[rows, :] = low
        own[rows, :] = (
            jnp.dot(context, w_out[...], preferred_element_type=jnp.float32)
            + lax.dot_general(low, up_out[...], CROSS, preferred_element_type=jnp.float32)
            + ffn[rows, :].astype(jnp.float32)
        ).astype(jnp.bfloat16)

    per = WORK_ROWS // LINE_CHUNK

    def prepare(at):
        @pl.when(lax.rem(at, per) == 0)
        def _():
            attend(at // per)

    def emit(rows, total):
        resid = start[rows, :].astype(jnp.float32) + total
        resid_out[rows, :] = resid
        normed = layer_norm(resid, gain[2:3, :], shift[2:3, :])
        final_out[rows, :] = normed.astype(jnp.bfloat16)

    line_sum(count, LINE_CHUNK, own, scratch[:4], scratch[4:8], prepare, emit)


def branch_kernel(
    count, raw, hits, stats, resid, gain, prompts, totals, out, loss_out, *scratch
):
    own, note_send, note_recv, scales, note_out, note_in = scratch[8:]
    me = lax.axis_index("mp")
    rows_all = raw.shape[0]
    greet_peers(me, count)
    note_send[...] = stats[...].T[0:8, :]
    copies = []
    for offset in range(1, count):
        copy = pltpu.make_async_remote_copy(
            src_ref=note_send,
            dst_ref=note_recv.at[offset],
            send_sem=note_out.at[offset],
            recv_sem=note_in.at[offset],
            device_id={"mp": lax.rem(me + offset, count)},
            device_id_type=MESH,
        )
        copy.start()
        copies.append(copy)
    mine = note_send[...]
    for copy in copies:
        copy.wait_recv()
    others = [mine] + [note_recv[offset] for offset in range(1, count)]
    top = functools.reduce(jnp.maximum, [part[0:1, :] for part in others])
    total = sum(part[1:2, :] * jnp.exp(part[0:1, :] - top) for part in others)
    found = sum(part[2:3, :] for part in others)
    spread_row = top + jnp.log(total)
    amount = sum(totals[e] - prompts[e] for e in range(prompts.shape[0]))
    example = lax.axis_index("dp")
    position = lax.broadcasted_iota(jnp.int32, (1, rows_all), 1)
    keep = (position >= prompts[example] - 1) & (position < totals[example] - 1)
    share = jnp.where(keep, 1.0 / jnp.broadcast_to(amount, (1, rows_all)).astype(jnp.float32), 0.0)
    loss_out[...] = (spread_row - found) * share
    factor = jnp.exp(mine[0:1, :] - spread_row) * share
    pair = jnp.concatenate([factor, share, jnp.zeros((126, rows_all), jnp.float32)], 0)
    scales[...] = pair.T

    def prepare(at):
        rows = line_chunk(at, LINE_CHUNK)
        scale = scales[rows, :]
        own[rows, :] = (
            raw[rows, :] * scale[:, 0:1] - hits[rows, :].astype(jnp.float32) * scale[:, 1:2]
        ).astype(jnp.bfloat16)

    def emit(rows, total):
        values = resid[rows, :]
        centre = values - jnp.mean(values, -1, keepdims=True)
        spread = jnp.mean(centre * centre, -1, keepdims=True)
        inverse = lax.rsqrt(spread + NORM_EPS)
        normed = centre * inverse
        up = total * gain[2:3, :]
        out[rows, :] = (
            inverse
            * (
                up
                - jnp.mean(up, -1, keepdims=True)
                - normed * jnp.mean(up * normed, -1, keepdims=True)
            )
        ).astype(jnp.bfloat16)

    line_sum(count, LINE_CHUNK, own, scratch[:4], scratch[4:8], prepare, emit, greet=False)
    for copy in copies:
        copy.wait_send()


def loss_kernel(vocab, tile, values, ahead, behind, hits, acc, stats, logits, probs, tops, sums):
    at = pl.program_id(0)
    tiles = pl.num_programs(0) - 1
    rows_all = values.shape[0]

    @pl.when(at == 0)
    def _():
        acc[...] = jnp.zeros_like(acc)
        tops[...] = jnp.full_like(tops, -1e29)
        sums[...] = jnp.zeros_like(sums)
        logits[...] = jnp.full_like(logits, -1e30)

    tail = vocab % tile
    if tail:

        @pl.when(at >= tiles - 1)
        def _():
            ahead[tail:, :] = jnp.zeros((tile - tail, ahead.shape[1]), ahead.dtype)

        @pl.when(at >= tiles)
        def _():
            behind[tail:, :] = jnp.zeros((tile - tail, behind.shape[1]), behind.dtype)

    ids = (at - 1) * tile + lax.broadcasted_iota(jnp.int32, (1, tile), 1)
    scores = logits[...] + jnp.where(ids < vocab, 0.0, -1e30)
    old = tops[:, 0:1]
    new = jnp.maximum(old, jnp.max(scores, -1, keepdims=True))
    weights = jnp.exp(scores - new)
    shrink = jnp.exp(old - new)
    sums[...] = sums[...] * shrink + jnp.sum(weights, -1, keepdims=True)
    tops[...] = jnp.broadcast_to(new, tops.shape)
    acc[...] = acc[...] * shrink
    probs[...] = weights.astype(jnp.bfloat16)
    logits[...] = lax.dot_general(
        values[...], ahead[...], (((1,), (1,)), ((), ())), preferred_element_type=jnp.float32
    )
    acc[...] += jnp.dot(probs[...], behind[...], preferred_element_type=jnp.float32)

    @pl.when(at == tiles)
    def _():
        found = jnp.sum(
            values[...].astype(jnp.float32) * hits[...].astype(jnp.float32), -1, keepdims=True
        )
        column = lax.broadcasted_iota(jnp.int32, (rows_all, 128), 1)
        stats[...] = jnp.where(
            column == 0, tops[...], jnp.where(column == 1, sums[...], found)
        )


LOSS_TILE = 512


def loss_call(values, head_rows, hits):
    rows, width = values.shape
    vocab = head_rows.shape[0]
    tile = LOSS_TILE
    tiles = pl.cdiv(vocab, tile)
    whole = pl.BlockSpec((rows, width), lambda j: (0, 0))
    return pl.pallas_call(
        functools.partial(loss_kernel, vocab, tile),
        name="loss",
        grid=(tiles + 1,),
        in_specs=[
            whole,
            pl.BlockSpec((tile, width), lambda j: (jnp.minimum(j, tiles - 1), 0)),
            pl.BlockSpec((tile, width), lambda j: (jnp.maximum(j - 1, 0), 0)),
            whole,
        ],
        out_specs=[whole, pl.BlockSpec((rows, 128), lambda j: (0, 0))],
        out_shape=[
            jax.ShapeDtypeStruct((rows, width), jnp.float32),
            jax.ShapeDtypeStruct((rows, 128), jnp.float32),
        ],
        scratch_shapes=[
            pltpu.VMEM((rows, tile), jnp.float32),
            pltpu.VMEM((rows, tile), jnp.bfloat16),
            pltpu.VMEM((rows, 128), jnp.float32),
            pltpu.VMEM((rows, 128), jnp.float32),
        ],
        compiler_params=pltpu.CompilerParams(vmem_limit_bytes=VMEM_LIMIT),
        cost_estimate=pl.CostEstimate(
            flops=4 * rows * width * vocab,
            bytes_accessed=4 * width * vocab,
            transcendentals=rows * vocab,
        ),
    )(values, head_rows, head_rows, hits)


def fold_kernel(splits, count, *refs):
    fulls = refs[0:4]
    groups = refs[4:8]
    losses, master, first, second, bases = refs[8:13]
    loss_out, norm_out, first_out, second_out, master_out = refs[13:18]
    scratch = refs[18:]
    sends = scratch[0:splits]
    recvs = scratch[splits : 2 * splits]
    keeps = scratch[2 * splits : 3 * splits]
    (line_send, line_recv, turn_send, turn_recv, note_send, note_recv, tell_send, tell_recv) = scratch[
        3 * splits : 3 * splits + 8
    ]
    (half_out, half_in, line_out, line_in, turn_out, turn_in, note_out, note_in, tell_out, tell_in) = (
        scratch[3 * splits + 8 :]
    )
    shards = 2**splits
    me = lax.axis_index("dp")
    lane = lax.axis_index("mp")
    full_rows = fulls[0].shape[0] // shards
    group_rows = groups[0].shape[0] // shards
    own_rows = full_rows // count
    bits = [(me // 2**k) % 2 for k in range(splits)]
    mates = [me + 2**k * (1 - 2 * bits[k]) for k in range(splits)]
    peers = [lax.rem(lane + offset, count) for offset in range(count)]
    spot = lane * shards + me
    goal = (spot // count, lax.rem(spot, count))
    place = me * count + lane
    origin = (lax.rem(place, shards), place // shards)
    moved = spot != place

    barrier = pltpu.get_barrier_semaphore()
    for mate in mates:
        pl.semaphore_signal(barrier, inc=1, device_id={"dp": mate, "mp": lane}, device_id_type=MESH)
    for peer in peers[1:]:
        pl.semaphore_signal(barrier, inc=1, device_id={"dp": me, "mp": peer}, device_id_type=MESH)

    @pl.when(moved)
    def _():
        for device in (goal, origin):
            pl.semaphore_signal(
                barrier, inc=1, device_id={"dp": device[0], "mp": device[1]}, device_id_type=MESH
            )

    pl.semaphore_wait(barrier, splits + count - 1 + jnp.where(moved, 2, 0))

    def remote(src, dst, out_sem, in_sem, device):
        return pltpu.make_async_remote_copy(
            src_ref=src,
            dst_ref=dst,
            send_sem=out_sem,
            recv_sem=in_sem,
            device_id={"dp": device[0], "mp": device[1]},
            device_id_type=MESH,
        )

    def piece(index):
        whole = pl.ds(pl.multiple_of(index * full_rows, full_rows), full_rows)
        part = pl.ds(pl.multiple_of(index * group_rows, group_rows), group_rows)
        return jnp.concatenate(
            [ref[whole, :] for ref in fulls] + [ref[part, :] for ref in groups], 0
        )

    started = []
    current = piece
    for k in range(splits):
        half = shards >> (k + 1)
        for i in range(half):
            sends[k][i] = current(2 * i + 1 - bits[k]).astype(jnp.bfloat16)
        copy = remote(sends[k], recvs[k], half_out.at[k], half_in.at[k], (mates[k], lane))
        copy.start()
        started.append(copy)
        for i in range(half):
            keeps[k][i] = current(2 * i + bits[k])
        copy.wait_recv()
        current = functools.partial(
            lambda kept, came, i: kept[i] + came[i].astype(jnp.float32), keeps[k], recvs[k]
        )
    final = keeps[splits - 1]
    final[0] = current(0)

    def chosen(peer):
        return jnp.concatenate(
            [
                final[
                    0,
                    pl.ds(pl.multiple_of(a * full_rows + peer * own_rows, own_rows), own_rows),
                    :,
                ]
                for a in range(4)
            ],
            0,
        )

    turn_send[...] = final[0, 4 * full_rows :, :].astype(jnp.bfloat16)
    turn = remote(turn_send, turn_recv, turn_out, turn_in, goal)

    @pl.when(moved)
    def _():
        turn.start()

    for offset in range(1, count):
        line_send[offset] = chosen(peers[offset]).astype(jnp.bfloat16)
        copy = remote(
            line_send.at[offset],
            line_recv.at[offset],
            line_out.at[offset],
            line_in.at[offset],
            (me, peers[offset]),
        )
        copy.start()
        started.append(copy)
    total = chosen(lane)

    @pl.when(moved)
    def _():
        turn.wait()

    @pl.when(jnp.logical_not(moved))
    def _():
        turn_recv[...] = turn_send[...]

    for copy in started[splits:]:
        copy.wait_recv()
    for offset in range(1, count):
        total = total + line_recv[offset].astype(jnp.float32)
    part = turn_recv[...].astype(jnp.float32)

    column = lax.broadcasted_iota(jnp.int32, (8, 128), 1)
    row = lax.broadcasted_iota(jnp.int32, (8, 128), 0)
    squares = jnp.sum(total * total) + jnp.sum(part * part)
    spot_norm = (row == 0) & (column == 0)
    spot_loss = (row == 0) & (column == 1)
    note = jnp.where(spot_norm, squares, 0.0) + jnp.where(spot_loss, jnp.sum(losses[...]), 0.0)

    def rows_of(index):
        source, slot = (total, (0, 1, 2, 7).index(index)) if index in (0, 1, 2, 7) else (
            part,
            index - 3,
        )
        return source[slot * own_rows : (slot + 1) * own_rows, :]

    turned = [
        jnp.dot(
            rows_of(m), bases[m], precision=HIGH_PRECISION, preferred_element_type=jnp.float32
        )
        for m in range(8)
    ]
    for k in range(splits):
        note_send[k] = note
        copy = remote(
            note_send.at[k], note_recv.at[k], note_out.at[k], note_in.at[k], (mates[k], lane)
        )
        copy.start()
        started.append(copy)
        copy.wait_recv()
        note = note + note_recv[k]
    tell_send[...] = note
    tells = []
    for offset in range(1, count):
        copy = remote(
            tell_send,
            tell_recv.at[offset],
            tell_out.at[offset],
            tell_in.at[offset],
            (me, peers[offset]),
        )
        copy.start()
        tells.append(copy)
    for copy in tells:
        copy.wait_recv()
    everything = note
    for offset in range(1, count):
        everything = everything + tell_recv[offset]
    norm = jnp.sqrt(jnp.sum(jnp.where(spot_norm, everything, 0.0), keepdims=True))
    loss_out[...] = jnp.sum(jnp.where(spot_loss, note, 0.0), keepdims=True)
    norm_out[...] = norm
    factor = jnp.minimum(1.0, CLIP_LIMIT / norm)
    for m in range(8):
        rotated = turned[m] * factor
        new_first = BETA_FIRST * first[m] + (1.0 - BETA_FIRST) * rotated
        new_second = BETA_SECOND * second[m] + (1.0 - BETA_SECOND) * rotated * rotated
        first_out[m] = new_first
        second_out[m] = new_second
        normed = (
            new_first
            / (1.0 - BETA_FIRST**ADAM_STEP)
            / (jnp.sqrt(new_second / (1.0 - BETA_SECOND**ADAM_STEP)) + ADAM_EPS)
        )
        back = lax.dot_general(
            normed,
            bases[m],
            (((1,), (1,)), ((), ())),
            precision=HIGH_PRECISION,
            preferred_element_type=jnp.float32,
        )
        master_out[m] = master[m] - LEARN_RATE * (back + DECAY_RATE * master[m])
    for copy in started + tells:
        copy.wait_send()


def fold_call(fulls, groups, losses, master, first_moment, second_moment, bases):
    shards = lax.axis_size("dp")
    count = lax.axis_size("mp")
    splits = shards.bit_length() - 1
    width = fulls[0].shape[1]
    pile = 4 * (fulls[0].shape[0] + groups[0].shape[0]) // shards
    own = 4 * fulls[0].shape[0] // (shards * count)
    low = jnp.bfloat16
    halves = [shards >> (k + 1) for k in range(splits)]
    dma = pltpu.SemaphoreType.DMA
    scratch = (
        [pltpu.VMEM((half, pile, width), low) for half in halves] * 2
        + [pltpu.VMEM((half, pile, width), jnp.float32) for half in halves]
        + [pltpu.VMEM((count, own, width), low)] * 2
        + [pltpu.VMEM((4 * groups[0].shape[0] // shards, width), low)] * 2
        + [pltpu.VMEM((splits, 8, 128), jnp.float32)] * 2
        + [pltpu.VMEM((8, 128), jnp.float32), pltpu.VMEM((count, 8, 128), jnp.float32)]
        + [dma((splits,))] * 2
        + [dma((count,))] * 2
        + [dma(())] * 2
        + [dma((splits,))] * 2
        + [dma((count,))] * 2
    )
    scalar = jax.ShapeDtypeStruct((1, 1), jnp.float32)
    state = jax.ShapeDtypeStruct(master.shape, jnp.float32)
    return line_call(
        functools.partial(fold_kernel, splits, count),
        "fold",
        3,
        [scalar, scalar, state, state, state],
        scratch,
        [*fulls, *groups, losses, master, first_moment, second_moment, bases],
    )


def per_device(
    token_ids,
    prompt_len,
    example_len,
    embedding,
    w_qkv,
    w_out,
    w_in,
    b_in,
    w_down,
    unembed,
    ln_gain,
    ln_bias,
    master,
    first_moment,
    second_moment,
    eigen_bases,
):
    group_count = lax.axis_size("mp")
    group_index = lax.axis_index("mp")
    head_rows = lax.all_gather(unembed.T, "dp", axis=1, tiled=True)
    examples, length = token_ids.shape
    width = embedding.shape[0]
    vocab_local = head_rows.shape[0]
    rows = examples * length
    local_heads = HEADS // group_count
    group_width = local_heads * HD
    flat_ids = token_ids.reshape(rows)
    picked = pick_call(flat_ids - group_index * width, embedding, "pick_start")
    shape_low = jax.ShapeDtypeStruct((rows, D), jnp.bfloat16)
    shape_wide = jax.ShapeDtypeStruct((rows, D), jnp.float32)
    shards = lax.axis_size("dp")
    own_rows = master.shape[1]
    pool_shape = (shards, group_count, 8, own_rows, R)
    start_rows, normed_attn, base, ffn_part, pool = line_call(
        functools.partial(start_kernel, group_count),
        "start_rows",
        0,
        [
            shape_low,
            shape_low,
            jax.ShapeDtypeStruct((rows, w_qkv.shape[1]), jnp.float32),
            shape_low,
            jax.ShapeDtypeStruct(pool_shape, jnp.bfloat16),
        ],
        line_scratch(rows, D)
        + [
            pltpu.VMEM((rows, D), jnp.bfloat16),
            pltpu.VMEM(w_qkv.shape, jnp.bfloat16),
            pltpu.VMEM(w_qkv.shape, jnp.bfloat16),
            pltpu.VMEM(w_in.shape, jnp.bfloat16),
            pltpu.VMEM(w_down.shape, jnp.bfloat16),
            pltpu.SemaphoreType.DMA((3,)),
            pltpu.VMEM(pool_shape, jnp.bfloat16),
        ]
        + [pltpu.SemaphoreType.DMA((group_count,))] * 2
        + [pltpu.SemaphoreType.DMA((shards - 1,))] * 2,
        [picked, ln_gain, ln_bias, b_in.reshape(1, -1), master, w_qkv, w_in, w_down],
        spaces=(pl.ANY,) * 3,
    )
    adapters = pool.transpose(2, 0, 1, 3, 4).reshape(8, -1, R)
    target = jnp.roll(token_ids, -1, axis=1).reshape(rows)
    adapter_rows = [
        lax.dynamic_slice_in_dim(
            adapters[3 + selector_index], group_index * group_width, group_width, 0
        )
        for selector_index in range(3)
    ]
    out_rows = lax.dynamic_slice_in_dim(adapters[6], group_index * group_width, group_width, 0)
    cosine, sine = rope_tables(length)
    rest = jnp.zeros((length, HD - ROT), jnp.float32)
    wide_cosine = jnp.concatenate([cosine[:, 0], cosine[:, 0], rest + 1.0] * (128 // HD), 1)
    wide_sine = jnp.concatenate([-sine[:, 0], sine[:, 0], rest] * (128 // HD), 1)
    shape_group = jax.ShapeDtypeStruct((rows, group_width), jnp.bfloat16)
    (
        inner,
        queries,
        key_rows,
        value_rows,
        context,
        spread_lanes,
        inner_out,
        resid,
        final_rows,
    ) = line_call(
        functools.partial(resid_kernel, group_count),
        "resid_rows",
        1,
        [
            jax.ShapeDtypeStruct((rows, 3 * R), jnp.bfloat16),
            shape_group,
            shape_group,
            shape_group,
            shape_group,
            jax.ShapeDtypeStruct((rows, 128), jnp.float32),
            jax.ShapeDtypeStruct((rows, R), jnp.bfloat16),
            shape_wide,
            shape_low,
        ],
        line_scratch(rows, D) + [pltpu.VMEM((rows, D), jnp.bfloat16)],
        [
            normed_attn,
            base,
            ffn_part,
            start_rows,
            ln_gain,
            ln_bias,
            wide_cosine,
            wide_sine,
            jnp.concatenate([adapters[0], adapters[1], adapters[2]], 1),
            *adapter_rows,
            out_rows,
            adapters[7],
            w_out,
        ],
    )
    queries = queries.reshape(1, length, local_heads, HD)
    key_rows = key_rows.reshape(1, length, local_heads, HD)
    value_rows = value_rows.reshape(1, length, local_heads, HD)
    spreads = [spread_lanes[:, :local_heads].T]
    goal = target - group_index * vocab_local
    hits = pick_call(goal, head_rows, "pick_target")
    raw_grad, stats = loss_call(final_rows, head_rows, hits)
    branch_grad, losses = line_call(
        functools.partial(branch_kernel, group_count),
        "branch_rows",
        2,
        [shape_low, jax.ShapeDtypeStruct((1, rows), jnp.float32)],
        line_scratch(rows, D)
        + [
            pltpu.VMEM((rows, D), jnp.bfloat16),
            pltpu.VMEM((8, rows), jnp.float32),
            pltpu.VMEM((group_count, 8, rows), jnp.float32),
            pltpu.VMEM((rows, 128), jnp.float32),
            pltpu.SemaphoreType.DMA((group_count,)),
            pltpu.SemaphoreType.DMA((group_count,)),
        ],
        [raw_grad, hits, stats, resid, ln_gain, prompt_len, example_len],
        spaces=(pltpu.SMEM,) * 2,
    )
    inner_out_grad = jnp.dot(branch_grad, adapters[7], preferred_element_type=jnp.float32).astype(
        jnp.bfloat16
    )
    grad_out_b = jnp.einsum("ld,lr->dr", branch_grad, inner_out, preferred_element_type=jnp.float32)
    grad_out_a = jnp.einsum(
        "ld,lr->dr", context, inner_out_grad, preferred_element_type=jnp.float32
    )
    context_grad = jnp.einsum(
        "ld,ed->le", branch_grad, w_out, preferred_element_type=jnp.float32
    ) + jnp.einsum("lr,dr->ld", inner_out_grad, out_rows, preferred_element_type=jnp.float32)
    context_grad = context_grad.astype(jnp.bfloat16).reshape(examples, length, local_heads, HD)
    sample = 0
    query_grad, key_grad, value_grad = attend_back(
        queries[sample], key_rows[sample], value_rows[sample], spreads[sample], context_grad[sample]
    )
    query_parts = [rotate_back(query_grad, cosine, sine)]
    key_parts = [rotate_back(key_grad, cosine, sine)]
    value_parts = [value_grad]
    pre_grads = [
        parts[0].reshape(rows, group_width).astype(jnp.bfloat16)
        for parts in (query_parts, key_parts, value_parts)
    ]
    complete_gradients = []
    local_grads = []
    for selector_index in range(3):
        projected_values = jnp.einsum(
            "ld,le->de", normed_attn, pre_grads[selector_index], preferred_element_type=jnp.float32
        )
        complete_gradients.append(
            jnp.dot(
                projected_values,
                adapter_rows[selector_index].astype(jnp.float32),
                precision=HIGH_PRECISION,
            )
        )
        local_grads.append(
            jnp.einsum(
                "ld,lr->dr",
                pre_grads[selector_index],
                inner[:, selector_index * R : (selector_index + 1) * R],
                preferred_element_type=jnp.float32,
            )
        )
    local_grads.append(grad_out_a)
    mean_loss, grad_norm, new_first, new_second, new_master = fold_call(
        [*complete_gradients, grad_out_b],
        local_grads,
        losses,
        master,
        first_moment,
        second_moment,
        eigen_bases,
    )
    return (mean_loss.reshape(()), grad_norm.reshape(()), new_first, new_second, new_master)


def solution(mesh):
    placed = (
        P("dp", None),
        P(),
        P(),
        P("mp", None),
        P(None, "mp"),
        P("mp", None),
        P(None, "mp"),
        P("mp"),
        P("mp", None),
        P("dp", "mp"),
        P(),
        P(),
        P(None, ("dp", "mp"), None),
        P(None, ("dp", "mp"), None),
        P(None, ("dp", "mp"), None),
        P(),
    )
    return jax.shard_map(
        per_device,
        mesh=mesh,
        in_specs=placed,
        out_specs=(
            P(),
            P(),
            P(None, ("dp", "mp"), None),
            P(None, ("dp", "mp"), None),
            P(None, ("dp", "mp"), None),
        ),
        check_vma=False,
    )
```

profile of v0, /device:TPU:0, one launch (start us, length us, event | category | flops | bytes accessed | tf_op | source)
XLA Modules:
  0.0 444.3 jit_solution(6362585915792240669)
XLA Ops:
  9.8 1.4 add_subtract_fusion
  11.5 2.0 fusion.34
  13.8 1.8 concatenate.32.cosine
  15.6 1.7 concatenate.33.sine
  19.1 14.7 %pick_start.1.part = bf16[1024,1024]{1,0:T(8,128)(2,1)} custom-call(s32[1024]{0:T(1024)} %fusion.49.spots, s32[1024,1]{1,0:T(8,128)} %fusion.30.places, bf16[12576,1024]{1,0:T(8,128)(2,1)} %table.1), custom_call_target="tpu_custom_call" | custom-call | flops 536870912 | bytes 16777216 | tf_op jit(solution)/shard_map/pick_start/pallas_call | solution.py:306
  33.8 74.2 %start_rows.1 = (bf16[1024,1024]{1,0:T(8,128)(2,1)}, bf16[1024,1024]{1,0:T(8,128)(2,1)}, f32[1024,768]{1,0:T(8,128)}, bf16[1024,1024]{1,0:T(8,128)(2,1)}, bf16[8,4,8,32,128]{4,3,2,1,0:T(8,128)(2,1)}) custom-call(bf16[1024,1024]{1,0:T(8,128)(2,1)} %pick_start.1.part, f32[3,1024]{1,0:T(4,128)} %gain.5, f32[3,1024]{1,0:T(4,128)} %shift.3, f32[1,1024]{1,0:T(1,128)} %bitcast.128, ...), custom_call_target="tpu_custom_call" | custom-call | bytes 119558400 | tf_op jit(solution)/shard_map/start_rows/pallas_call | solution.py:346
  108.0 2.6 fusion.63
  114.1 73.6 %resid_rows.1 = (bf16[1024,384]{1,0:T(8,128)(2,1)}, bf16[1024,256]{1,0:T(8,128)(2,1)}, bf16[1024,256]{1,0:T(8,128)(2,1)}, bf16[1024,256]{1,0:T(8,128)(2,1)}, bf1...) custom-call(bf16[1024,1024]{1,0:T(8,128)(2,1)} %get-tuple-element.92, ...), custom_call_target="tpu_custom_call" | custom-call | bytes 122306816 | tf_op jit(solution)/shard_map/resid_rows/pallas_call | solution.py:346
  188.8 1.2 copy.77
  198.4 2.7 fusion.67
  201.1 4.5 %fusion.69 = f32[4,512,1024]{2,1,0:T(8,128)} fusion(bf16[512,4,64]{0,2,1:T(8,128)(2,1)S(1)} %bitcast.100, bf16[1024,4,64]{0,2,1:T(8,128)(2,1)S(1)} %bitcast.93), kind=kOutput, calls=%fused_computation.112 | convolution fusion | flops 268435456 | bytes 9175040 | tf_op jit(solution)/shard_map/qhd,khd->hqk/dot_general | solution.py:55
  205.7 14.5 %pick_target.1.hits = bf16[1024,1024]{1,0:T(8,128)(2,1)} custom-call(s32[1024]{0:T(1024)} %fusion.51.spots, s32[1024,1]{1,0:T(8,128)} %fusion.33.places, bf16[12576,1024]{1,0:T(8,128)(2,1)} %all-gather.2.cloned.1.call-done.table.ahead.behind), custom_call_target="tpu_custom_call" | custom-call | flops 536870912 | bytes 16777216 | tf_op jit(solution)/shard_map/pick_target/pallas_call | solution.py:306
  220.2 71.4 %loss.1 = (f32[1024,1024]{1,0:T(8,128)}, f32[1024,128]{1,0:T(8,128)}) custom-call(bf16[1024,1024]{1,0:T(8,128)(2,1)} %get-tuple-element.100.values, bf16[12576,1024]{1,0:T(8,128)(2,1)} %all-gather.2.cloned.1.call-done.table.ahead.behind, bf16[12576,1024]{1,0:T(8,128)(2,1)} %all-gather.2.cloned.1.call-done.table.ahead.behind, bf16[1024,1024]{1,0:T(8,128)(2,1)} %pick_target.1.hits), custom_call_target="tpu_custom_call" | custom-call | flops 52747567104 | bytes 51511296 | tf_op jit(solution)/shard_map/loss/pallas_call | solution.py:765
  291.6 65.0 %branch_rows.1 = (bf16[1024,1024]{1,0:T(8,128)(2,1)}, f32[1,1024]{1,0:T(1,128)}) custom-call(f32[1024,1024]{1,0:T(8,128)} %get-tuple-element.101.raw, bf16[1024,1024]{1,0:T(8,128)(2,1)} %pick_target.1.hits, f32[1024,128]{1,0:T(8,128)} %get-tuple-element.102.stats, f32[1024,1024]{1,0:T(8,128)} %get-tuple-element.103.resid, f32[3,1024]{1,0:T(4,128)} %gain.5, ...), custom_call_target="tpu_custom_call" | custom-call | bytes 113123648 | tf_op jit(solution)/shard_map/branch_rows/pallas_call | solution.py:346
  356.6 2.3 convolution_convert_fusion
  359.0 2.5 fusion.68
  361.8 1.3 fusion.20
  363.1 1.5 multiply_reduce_fusion.1
  364.7 1.3 multiply_convert_fusion.1
  367.2 2.5 fusion.16
  370.5 1.9 fusion.39.refs_6_
  372.4 3.2 multiply_reduce_fusion
  375.5 2.6 multiply_convert_fusion
  378.2 1.4 fusion.23
  386.1 1.6 fusion.76.refs_3_
  387.7 1.4 fusion.75.refs_2_
  389.1 1.4 fusion.73.refs_1_
  390.5 1.4 fusion.71.refs_0_
  391.9 36.7 %fold.1 = (f32[1,1]{1,0:T(1,128)}, f32[1,1]{1,0:T(1,128)}, f32[8,32,128]{2,1,0:T(8,128)}, f32[8,32,128]{2,1,0:T(8,128)}, f32[8,32,128]{2,1,0:T(8,128)}) custom-call(f32[1024,128]{1,0:T(8,128)} %fusion.71.refs_0_, f32[1024,128]{1,0:T(8,128)} %fusion.73.refs_1_, f32[1024,128]{1,0:T(8,128)} %fusion.75.refs_2_, f32[1024,128]{1,0:T(8,128)} %fusion.76.refs_3_, ...), custom_call_target="tpu_custom_call" | custom-call | bytes 103936264 | tf_op jit(solution)/shard_map/fold/pallas_call | solution.py:346
  430.1 1.6 copy.95
  431.6 1.6 copy.96
  433.2 1.6 copy.97
  (83 shorter events, 26.6 us)
Async XLA Ops:
  7.2 198.5 %all-gather.2.cloned.1.call-start = ((), (), s32[]{:S(2)}) async-start(), calls=%async_computation | async-start | bytes 28975104 | tf_op jit(solution)/shard_map/all_gather | solution.py:1050
  291.6 65.0 %copy-start.3 = (bf16[1,8,4,32,128]{4,3,0,2,1:T(8,128)(2,1)S(1)}, bf16[1,8,4,32,128]{4,3,0,2,1:T(8,128)(2,1)}, u32[]{:S(2)}) copy-start(bf16[1,8,4,32,128]{4,3,0,2,1:T(8,128)(2,1)} %get-tuple-element.115) | copy-start | bytes 786436
  291.6 67.3 %copy-start.4 = (bf16[256,1024]{1,0:T(8,128)(2,1)S(1)}, bf16[256,1024]{1,0:T(8,128)(2,1)}, u32[]{:S(2)}) copy-start(bf16[256,1024]{1,0:T(8,128)(2,1)} %w_out.1) | copy-start | bytes 1572868
  356.6 4.9 %copy-start.10 = (bf16[256,128]{1,0:T(8,128)(2,1)S(1)}, bf16[256,128]{1,0:T(8,128)(2,1)}, u32[]{:S(2)}) copy-start(bf16[256,128]{1,0:T(8,128)(2,1)} %constant_dynamic-slice_fusion.down_out) | copy-start | bytes 196612
  359.0 2.9 copy-start.2
  361.5 1.6 copy-start.5
  363.1 4.1 slice-start
  364.7 2.5 slice-start.1
  367.2 2.5 copy-start
  380.5 1.1 copy-start.6
  383.3 1.8 copy-start.11
  383.3 2.8 copy-start.1
  383.3 2.8 copy-start.12
  385.1 2.6 copy-start.9
  385.1 4.0 copy-start.8
  386.1 4.4 copy-start.7
Sparse Core Ops, SparseCore 0:
  9.8 141.1 all-gather.1
where the time goes:
time: 451 us; the launch traced here: 444 us
  Pallas kernels  350 us (78%)
  matrix products  37.2 us (8%)
  local copies, waits for them, and re-layouts  25.3 us (6%)
  between operations  18.5 us (4%)
  other arithmetic  12.4 us (3%)
    pallas_call x4, Pallas kernels, line_call(): pl.pallas_call(kernel, name=name, out_shape=outs, in_specs=[vmem] * (len(...  250 us
    pallas_call x1, Pallas kernels, loss_call(): pl.pallas_call(functools.partial(loss_kernel, vocab, tile), name='loss',...  71.4 us
    pallas_call x2, Pallas kernels, pick_call(): pl.pallas_call(pick_kernel, name=name, in_specs=[pl.BlockSpec(memory_spac...  29.2 us
  transfers between devices with their start and end apart: 1, of which 0 were waited for; matrix products, arithmetic and copies ran while one was open for 8% of the time, Pallas kernels for 37%

commit v1 on v0

--- a/solution.py
+++ b/solution.py
@@ -40,70 +40,6 @@
     freqs = ROPE_BASE ** (-2.0 * jnp.arange(half, dtype=jnp.float32) / ROT)
     angles = jnp.arange(length, dtype=jnp.float32)[:, None] * freqs[None, :]
     return (jnp.cos(angles)[:, None, :], jnp.sin(angles)[:, None, :])
-
-
-def rotate_back(upstream, cosine, sine):
-    half = ROT // 2
-    first = upstream[..., :half]
-    second = upstream[..., half:ROT]
-    return jnp.concatenate(
-        [first * cosine + second * sine, second * cosine - first * sine, upstream[..., ROT:]], -1
-    )
-
-
-def masked_scores(queries, key_rows, start_row, stop_row):
-    scores = jnp.einsum(
-        "qhd,khd->hqk",
-        queries[start_row:stop_row],
-        key_rows[:stop_row],
-        preferred_element_type=jnp.float32,
-    ) * HD ** (-0.5)
-    query_pos = start_row + jnp.arange(stop_row - start_row)[:, None]
-    causal = jnp.arange(stop_row)[None, :] <= query_pos
-    return jnp.where(causal[None], scores, -1e30)
-
-
-def attend_back(queries, key_rows, value_rows, spreads, upstream):
-    length = queries.shape[0]
-    row_block = min(512, length)
-    scaling = HD ** (-0.5)
-    query_grads = []
-    key_grad = jnp.zeros(key_rows.shape, jnp.float32)
-    value_grad = jnp.zeros(value_rows.shape, jnp.float32)
-    for start_row in range(0, length, row_block):
-        stop_row = start_row + row_block
-        scores = masked_scores(queries, key_rows, start_row, stop_row)
-        probs = jnp.exp(scores - spreads[:, start_row:stop_row, None])
-        grad_here = upstream[start_row:stop_row]
-        prob_grad = jnp.einsum(
-            "qhd,khd->hqk", grad_here, value_rows[:stop_row], preferred_element_type=jnp.float32
-        )
-        inner_sum = jnp.sum(probs * prob_grad, -1, keepdims=True)
-        score_grad = (probs * (prob_grad - inner_sum)).astype(jnp.bfloat16)
-        query_grads.append(
-            jnp.einsum(
-                "hqk,khd->qhd", score_grad, key_rows[:stop_row], preferred_element_type=jnp.float32
-            )
-            * scaling
-        )
-        key_grad = key_grad.at[:stop_row].add(
-            jnp.einsum(
-                "hqk,qhd->khd",
-                score_grad,
-                queries[start_row:stop_row],
-                preferred_element_type=jnp.float32,
-            )
-            * scaling
-        )
-        value_grad = value_grad.at[:stop_row].add(
-            jnp.einsum(
-                "hqk,qhd->khd",
-                probs.astype(jnp.bfloat16),
-                grad_here,
-                preferred_element_type=jnp.float32,
-            )
-        )
-    return (jnp.concatenate(query_grads, 0), key_grad, value_grad)
 
 
 def line_chunk(index, size):
@@ -638,12 +574,45 @@
     line_sum(count, LINE_CHUNK, own, scratch[:4], scratch[4:8], prepare, emit)
 
 
-def branch_kernel(
-    count, raw, hits, stats, resid, gain, prompts, totals, out, loss_out, *scratch
-):
-    own, note_send, note_recv, scales, note_out, note_in = scratch[8:]
+DOWN = (((0,), (0,)), ((), ()))
+
+
+def branch_kernel(count, raw, hits, stats, gain, up_q, up_k, up_v, down_out, *refs):
+    prompts, totals = refs[0:2]
+    sources = refs[2:15]
+    loss_out = refs[15]
+    grad_down = refs[16:19]
+    grad_out_b = refs[19]
+    grad_up = refs[20:23]
+    grad_out_a = refs[23]
+    scratch = refs[24:]
+    own, note_send, note_recv, scales, note_out, note_in = scratch[8:14]
+    held = scratch[14:27]
+    sems, out, query_grad, key_turned, value_turned, out_b_turned, out_a_turned = scratch[27:]
+    (
+        resid,
+        queries,
+        keys,
+        values,
+        context,
+        spreads,
+        inner,
+        low,
+        attn,
+        w_out,
+        up_out,
+        cosine,
+        sine,
+    ) = held
     me = lax.axis_index("mp")
     rows_all = raw.shape[0]
+    group = w_out.shape[0]
+    loads = [
+        pltpu.make_async_copy(src, dst, sems.at[slot])
+        for slot, (src, dst) in enumerate(zip(sources, held))
+    ]
+    for load in loads:
+        load.start()
     greet_peers(me, count)
     note_send[...] = stats[...].T[0:8, :]
     copies = []
@@ -658,6 +627,8 @@
         )
         copy.start()
         copies.append(copy)
+    for ref in (key_turned, value_turned, out_b_turned, out_a_turned):
+        ref[...] = jnp.zeros_like(ref)
     mine = note_send[...]
     for copy in copies:
         copy.wait_recv()
@@ -675,6 +646,8 @@
     factor = jnp.exp(mine[0:1, :] - spread_row) * share
     pair = jnp.concatenate([factor, share, jnp.zeros((126, rows_all), jnp.float32)], 0)
     scales[...] = pair.T
+    for load in loads:
+        load.wait()
 
     def prepare(at):
         rows = line_chunk(at, LINE_CHUNK)
@@ -684,8 +657,8 @@
         ).astype(jnp.bfloat16)
 
     def emit(rows, total):
-        values = resid[rows, :]
-        centre = values - jnp.mean(values, -1, keepdims=True)
+        values_here = resid[rows, :]
+        centre = values_here - jnp.mean(values_here, -1, keepdims=True)
         spread = jnp.mean(centre * centre, -1, keepdims=True)
         inverse = lax.rsqrt(spread + NORM_EPS)
         normed = centre * inverse
@@ -699,7 +672,105 @@
             )
         ).astype(jnp.bfloat16)
 
-    line_sum(count, LINE_CHUNK, own, scratch[:4], scratch[4:8], prepare, emit, greet=False)
+    def attend_back(block):
+        rows = line_chunk(block, WORK_ROWS)
+        upstream = out[rows, :]
+        low_grad = jnp.dot(upstream, up_out[...], preferred_element_type=jnp.float32).astype(
+            jnp.bfloat16
+        )
+        grads = (
+            lax.dot_general(upstream, w_out[...], CROSS, preferred_element_type=jnp.float32)
+            + lax.dot_general(low_grad, down_out[...], CROSS, preferred_element_type=jnp.float32)
+        ).astype(jnp.bfloat16)
+        out_b_turned[...] += lax.dot_general(
+            low[rows, :], upstream, DOWN, preferred_element_type=jnp.float32
+        )
+        out_a_turned[...] += lax.dot_general(
+            low_grad, context[rows, :], DOWN, preferred_element_type=jnp.float32
+        )
+        lane = lax.broadcasted_iota(jnp.int32, (WORK_ROWS, 128), 1)
+        column = lax.broadcasted_iota(jnp.int32, (WORK_ROWS, rows_all), 1)
+        place = lax.broadcasted_iota(jnp.int32, (WORK_ROWS, rows_all), 0)
+        seen = column <= place + block * WORK_ROWS
+        for at in range(0, group, 128):
+            pick = slice(at, at + 128)
+            joined = jnp.zeros((WORK_ROWS, 128), jnp.float32)
+            key_part = jnp.zeros((128, rows_all), jnp.float32)
+            value_part = jnp.zeros((128, rows_all), jnp.float32)
+            for side in range(128 // HD):
+                head = at // HD + side
+                here = lane // HD == side
+                query = jnp.where(here, queries[rows, pick], jnp.zeros((), jnp.bfloat16))
+                grad = jnp.where(here, grads[:, pick], jnp.zeros((), jnp.bfloat16))
+                scores = (
+                    lax.dot_general(
+                        query, keys[:, pick], CROSS, preferred_element_type=jnp.float32
+                    )
+                    * HD**-0.5
+                )
+                scores = jnp.where(seen, scores, -1e30)
+                probs = jnp.exp(scores - spreads[rows, head : head + 1])
+                prob_grad = lax.dot_general(
+                    grad, values[:, pick], CROSS, preferred_element_type=jnp.float32
+                )
+                mean = jnp.sum(probs * prob_grad, -1, keepdims=True)
+                score_grad = (probs * (prob_grad - mean)).astype(jnp.bfloat16)
+                result = jnp.dot(score_grad, keys[:, pick], preferred_element_type=jnp.float32)
+                joined = jnp.where(here, result, joined)
+                key_part += lax.dot_general(
+                    query, score_grad, DOWN, preferred_element_type=jnp.float32
+                )
+                value_part += lax.dot_general(
+                    grad, probs.astype(jnp.bfloat16), DOWN, preferred_element_type=jnp.float32
+                )
+            key_turned[pick, :] += key_part
+            value_turned[pick, :] += value_part
+            query_grad[rows, pick] = turn_pairs(
+                joined * HD**-0.5, cosine[rows, :], sine[rows, :], -1.0
+            ).astype(jnp.bfloat16)
+
+    per = WORK_ROWS // LINE_CHUNK
+
+    def follow(ready):
+        @pl.when(lax.rem(ready, per) == per - 1)
+        def _():
+            attend_back(ready // per)
+
+    line_sum(
+        count,
+        LINE_CHUNK,
+        own,
+        scratch[:4],
+        scratch[4:8],
+        prepare,
+        emit,
+        greet=False,
+        follow=follow,
+    )
+    key_grad = jnp.concatenate(
+        [
+            turn_pairs(
+                key_turned[at : at + 128, :].T * HD**-0.5, cosine[...], sine[...], -1.0
+            ).astype(jnp.bfloat16)
+            for at in range(0, group, 128)
+        ],
+        1,
+    )
+    value_grad = value_turned[...].T.astype(jnp.bfloat16)
+    for kind, (grad, up) in enumerate(
+        ((query_grad[...], up_q), (key_grad, up_k), (value_grad, up_v))
+    ):
+        wide = jnp.dot(grad, up[...], preferred_element_type=jnp.float32)
+        high = wide.astype(jnp.bfloat16)
+        rest = (wide - high.astype(jnp.float32)).astype(jnp.bfloat16)
+        turned = lax.dot_general(high, attn[...], DOWN, preferred_element_type=jnp.float32)
+        turned += lax.dot_general(rest, attn[...], DOWN, preferred_element_type=jnp.float32)
+        grad_down[kind][...] = turned.T
+        grad_up[kind][...] = lax.dot_general(
+            inner[:, kind * R : (kind + 1) * R], grad, DOWN, preferred_element_type=jnp.float32
+        ).T
+    grad_out_b[...] = out_b_turned[...].T
+    grad_out_a[...] = out_a_turned[...].T
     for copy in copies:
         copy.wait_send()
 
@@ -1143,18 +1214,31 @@
             w_out,
         ],
     )
-    queries = queries.reshape(1, length, local_heads, HD)
-    key_rows = key_rows.reshape(1, length, local_heads, HD)
-    value_rows = value_rows.reshape(1, length, local_heads, HD)
-    spreads = [spread_lanes[:, :local_heads].T]
     goal = target - group_index * vocab_local
     hits = pick_call(goal, head_rows, "pick_target")
     raw_grad, stats = loss_call(final_rows, head_rows, hits)
-    branch_grad, losses = line_call(
+    late = [
+        resid,
+        queries,
+        key_rows,
+        value_rows,
+        context,
+        spread_lanes,
+        inner,
+        inner_out,
+        normed_attn,
+        w_out,
+        adapters[7],
+        wide_cosine,
+        wide_sine,
+    ]
+    tall = jax.ShapeDtypeStruct((D, R), jnp.float32)
+    short = jax.ShapeDtypeStruct((group_width, R), jnp.float32)
+    losses, grad_q, grad_k, grad_v, grad_out_b, *local_grads = line_call(
         functools.partial(branch_kernel, group_count),
         "branch_rows",
         2,
-        [shape_low, jax.ShapeDtypeStruct((1, rows), jnp.float32)],
+        [jax.ShapeDtypeStruct((1, rows), jnp.float32)] + [tall] * 4 + [short] * 4,
         line_scratch(rows, D)
         + [
             pltpu.VMEM((rows, D), jnp.bfloat16),
@@ -1163,56 +1247,32 @@
             pltpu.VMEM((rows, 128), jnp.float32),
             pltpu.SemaphoreType.DMA((group_count,)),
             pltpu.SemaphoreType.DMA((group_count,)),
+        ]
+        + [pltpu.VMEM(value.shape, value.dtype) for value in late]
+        + [
+            pltpu.SemaphoreType.DMA((len(late),)),
+            pltpu.VMEM((rows, D), jnp.bfloat16),
+            pltpu.VMEM((rows, group_width), jnp.bfloat16),
+            pltpu.VMEM((group_width, rows), jnp.float32),
+            pltpu.VMEM((group_width, rows), jnp.float32),
+            pltpu.VMEM((R, D), jnp.float32),
+            pltpu.VMEM((R, group_width), jnp.float32),
         ],
-        [raw_grad, hits, stats, resid, ln_gain, prompt_len, example_len],
-        spaces=(pltpu.SMEM,) * 2,
-    )
-    inner_out_grad = jnp.dot(branch_grad, adapters[7], preferred_element_type=jnp.float32).astype(
-        jnp.bfloat16
-    )
-    grad_out_b = jnp.einsum("ld,lr->dr", branch_grad, inner_out, preferred_element_type=jnp.float32)
-    grad_out_a = jnp.einsum(
-        "ld,lr->dr", context, inner_out_grad, preferred_element_type=jnp.float32
-    )
-    context_grad = jnp.einsum(
-        "ld,ed->le", branch_grad, w_out, preferred_element_type=jnp.float32
-    ) + jnp.einsum("lr,dr->ld", inner_out_grad, out_rows, preferred_element_type=jnp.float32)
-    context_grad = context_grad.astype(jnp.bfloat16).reshape(examples, length, local_heads, HD)
-    sample = 0
-    query_grad, key_grad, value_grad = attend_back(
-        queries[sample], key_rows[sample], value_rows[sample], spreads[sample], context_grad[sample]
-    )
-    query_parts = [rotate_back(query_grad, cosine, sine)]
-    key_parts = [rotate_back(key_grad, cosine, sine)]
-    value_parts = [value_grad]
-    pre_grads = [
-        parts[0].reshape(rows, group_width).astype(jnp.bfloat16)
-        for parts in (query_parts, key_parts, value_parts)
-    ]
-    complete_gradients = []
-    local_grads = []
-    for selector_index in range(3):
-        projected_values = jnp.einsum(
-            "ld,le->de", normed_attn, pre_grads[selector_index], preferred_element_type=jnp.float32
-        )
-        complete_gradients.append(
-            jnp.dot(
-                projected_values,
-                adapter_rows[selector_index].astype(jnp.float32),
-                precision=HIGH_PRECISION,
-            )
-        )
-        local_grads.append(
-            jnp.einsum(
-                "ld,lr->dr",
-                pre_grads[selector_index],
-                inner[:, selector_index * R : (selector_index + 1) * R],
-                preferred_element_type=jnp.float32,
-            )
-        )
-    local_grads.append(grad_out_a)
+        [
+            raw_grad,
+            hits,
+            stats,
+            ln_gain,
+            *adapter_rows,
+            out_rows,
+            prompt_len,
+            example_len,
+            *late,
+        ],
+        spaces=(pltpu.SMEM,) * 2 + (pl.ANY,) * len(late),
+    )
     mean_loss, grad_norm, new_first, new_second, new_master = fold_call(
-        [*complete_gradients, grad_out_b],
+        [grad_q, grad_k, grad_v, grad_out_b],
         local_grads,
         losses,
         master,

time: 451 us -> 405 us (0.90); the launches traced: 444 us -> 405 us
  matrix products: 37.2 us -> 0 us
  Pallas kernels: 350 us -> 365 us
  local copies, waits for them, and re-layouts: 25.3 us -> 14.4 us
  other arithmetic: 12.4 us -> 7.15 us
    dot_general x24 -> x0, matrix products: 37.2 us -> none  [the longest x2 7.28 us: masked_scores(): jnp.einsum('qhd,khd->hqk', queries[start_row:stop_row], key_rows[:stop_ro...]
    pallas_call x4, Pallas kernels: 250 us -> 264 us  [line_call(): pl.pallas_call(kernel, name=name, out_shape=outs, in_specs=[vmem] * (len(...]
    slice x12 -> x0, local copies, waits for them, and re-layouts: 4.62 us -> none  [the longest x2 1.81 us: attend_back(): value_rows[:stop_row]]
  transfers between devices with their start and end apart: 1 -> 1, of which waited for: 0 -> 0; matrix products, arithmetic and copies ran while one was open for 8% -> 4% of each run, Pallas kernels for 37% -> 40%
where the time goes in v1:
time: 405 us
  Pallas kernels  365 us (90%)
  between operations  17.6 us (4%)
  local copies, waits for them, and re-layouts  14.4 us (4%)
  other arithmetic  7.15 us (2%)
    pallas_call x4, Pallas kernels, line_call(): pl.pallas_call(kernel, name=name, out_shape=outs, in_specs=[vmem] * (len(...  264 us
    pallas_call x1, Pallas kernels, loss_call(): pl.pallas_call(functools.partial(loss_kernel, vocab, tile), name='loss',...  71.6 us
    pallas_call x2, Pallas kernels, pick_call(): pl.pallas_call(pick_kernel, name=name, in_specs=[pl.BlockSpec(memory_spac...  29.1 us
  transfers between devices with their start and end apart: 1, of which 0 were waited for; matrix products, arithmetic and copies ran while one was open for 4% of the time, Pallas kernels for 40%

profile of v1, /device:TPU:0, one launch (start us, length us, event | category | flops | bytes accessed | tf_op | source)
XLA Modules:
  0.0 404.6 jit_solution(13586575716038671584)
XLA Ops:
  7.2 0.0 copy-start
  7.2 0.0 all-gather.2.cloned.1.call-start
  7.2 0.7 all-gather.2.cloned.1.call-update
  7.9 0.0 copy-done
  7.9 0.1 slice.49
  8.0 0.5 slice.50
  8.5 0.7 add_subtract_fusion
  9.2 0.2 copy.31
  9.5 0.2 copy.37
  9.7 2.0 fusion.7
  11.7 1.8 concatenate.13.cosine.refs_13_
  13.5 1.8 concatenate.14.sine.refs_14_
  15.3 0.6 fusion.14.spots
  15.9 1.1 fusion.3.places
  17.0 14.5 %pick_start.1.part = bf16[1024,1024]{1,0:T(8,128)(2,1)} custom-call(s32[1024]{0:T(1024)} %fusion.14.spots, s32[1024,1]{1,0:T(8,128)} %fusion.3.places, bf16[12576,1024]{1,0:T(8,128)(2,1)} %table.1), custom_call_target="tpu_custom_call" | custom-call | flops 536870912 | bytes 16777216 | tf_op jit(solution)/shard_map/pick_start/pallas_call | solution.py:242
  31.6 74.3 %start_rows.1 = (bf16[1024,1024]{1,0:T(8,128)(2,1)}, bf16[1024,1024]{1,0:T(8,128)(2,1)}, f32[1024,768]{1,0:T(8,128)}, bf16[1024,1024]{1,0:T(8,128)(2,1)}, bf16[8,4,8,32,128]{4,3,2,1,0:T(8,128)(2,1)}) custom-call(bf16[1024,1024]{1,0:T(8,128)(2,1)} %pick_start.1.part, f32[3,1024]{1,0:T(4,128)} %gain.5, f32[3,1024]{1,0:T(4,128)} %shift.3, f32[1,1024]{1,0:T(1,128)} %bitcast.32, ...), custom_call_target="tpu_custom_call" | custom-call | bytes 119558400 | tf_op jit(solution)/shard_map/start_rows/pallas_call | solution.py:282
  105.9 2.6 fusion.24
  108.5 0.6 constant_dynamic-slice_fusion.down_out
  109.1 0.6 constant_dynamic-slice_fusion.1.up_v
  109.7 0.6 constant_dynamic-slice_fusion.2.up_k
  110.4 0.6 constant_dynamic-slice_fusion.3.up_q
  111.0 1.0 pad_maximum_fusion.down_qkv
  112.0 74.0 %resid_rows.1 = (bf16[1024,384]{1,0:T(8,128)(2,1)}, bf16[1024,256]{1,0:T(8,128)(2,1)}, bf16[1024,256]{1,0:T(8,128)(2,1)}, bf16[1024,256]{1,0:T(8,128)(2,1)}, bf1...) custom-call(bf16[1024,1024]{1,0:T(8,128)(2,1)} %get-tuple-element.35, ...), custom_call_target="tpu_custom_call" | custom-call | bytes 122306816 | tf_op jit(solution)/shard_map/resid_rows/pallas_call | solution.py:282
  186.1 0.6 fusion.16.spots
  186.7 1.1 fusion.6.places
  187.8 14.6 %pick_target.1.hits = bf16[1024,1024]{1,0:T(8,128)(2,1)} custom-call(s32[1024]{0:T(1024)} %fusion.16.spots, s32[1024,1]{1,0:T(8,128)} %fusion.6.places, bf16[12576,1024]{1,0:T(8,128)(2,1)} %all-gather.2.cloned.1.call-done.table.ahead.behind), custom_call_target="tpu_custom_call" | custom-call | flops 536870912 | bytes 16777216 | tf_op jit(solution)/shard_map/pick_target/pallas_call | solution.py:242
  202.4 71.6 %loss.1 = (f32[1024,1024]{1,0:T(8,128)}, f32[1024,128]{1,0:T(8,128)}) custom-call(bf16[1024,1024]{1,0:T(8,128)(2,1)} %get-tuple-element.40.values, bf16[12576,1024]{1,0:T(8,128)(2,1)} %all-gather.2.cloned.1.call-done.table.ahead.behind, bf16[12576,1024]{1,0:T(8,128)(2,1)} %all-gather.2.cloned.1.call-done.table.ahead.behind, bf16[1024,1024]{1,0:T(8,128)(2,1)} %pick_target.1.hits), custom_call_target="tpu_custom_call" | custom-call | flops 52747567104 | bytes 51511296 | tf_op jit(solution)/shard_map/loss/pallas_call | solution.py:836
  274.0 79.3 %branch_rows.1 = (f32[1,1024]{1,0:T(1,128)}, f32[1024,128]{1,0:T(8,128)}, f32[1024,128]{1,0:T(8,128)}, f32[1024,128]{1,0:T(8,128)}, f32[1024,128]{1,0:T(8,128)},...) custom-call(f32[1024,1024]{1,0:T(8,128)} %get-tuple-element.41.raw, ...), custom_call_target="tpu_custom_call" | custom-call | bytes 121512256 | tf_op jit(solution)/shard_map/branch_rows/pallas_call | solution.py:282
  353.3 36.2 %fold.1 = (f32[1,1]{1,0:T(1,128)}, f32[1,1]{1,0:T(1,128)}, f32[8,32,128]{2,1,0:T(8,128)}, f32[8,32,128]{2,1,0:T(8,128)}, f32[8,32,128]{2,1,0:T(8,128)}) custom-call(f32[1024,128]{1,0:T(8,128)} %get-tuple-element.51.refs_0_, f32[1024,128]{1,0:T(8,128)} %get-tuple-element.52.refs_1_, f32[1024,128]{1,0:T(8,128)} %get-tuple-element.53.refs_2_, ...), custom_call_target="tpu_custom_call" | custom-call | bytes 103936264 | tf_op jit(solution)/shard_map/fold/pallas_call | solution.py:282
  390.8 1.6 copy.49
  392.4 1.6 copy.50
  393.9 1.6 copy.51
  (4 shorter events, 0.1 us)
Async XLA Ops:
  7.2 0.8 copy-start
  7.2 180.6 %all-gather.2.cloned.1.call-start = ((), (), s32[]{:S(2)}) async-start(), calls=%async_computation | async-start | bytes 28975104 | tf_op jit(solution)/shard_map/all_gather | solution.py:1121
Sparse Core Ops, SparseCore 0:
  9.9 141.1 all-gather.1

commit v2 on v1

--- a/solution.py
+++ b/solution.py
@@ -46,25 +46,6 @@
     return pl.ds(pl.multiple_of(index * size, size), size)
 
 
-def greet_line(me, count):
-    barrier = pltpu.get_barrier_semaphore()
-
-    @pl.when(me > 0)
-    def _():
-        pl.semaphore_signal(
-            barrier, inc=1, device_id={"mp": jnp.maximum(me - 1, 0)}, device_id_type=MESH
-        )
-
-    @pl.when(me < count - 1)
-    def _():
-        pl.semaphore_signal(
-            barrier, inc=1, device_id={"mp": jnp.minimum(me + 1, count - 1)}, device_id_type=MESH
-        )
-
-    peers = jnp.where(me > 0, 1, 0) + jnp.where(me < count - 1, 1, 0)
-    pl.semaphore_wait(barrier, peers)
-
-
 def greet_peers(me, count):
     barrier = pltpu.get_barrier_semaphore()
     for offset in range(1, count):
@@ -74,7 +55,7 @@
     pl.semaphore_wait(barrier, count - 1)
 
 
-def line_sum(count, chunk, own, wires, sems, prepare, emit, greet=True, follow=None, always=False):
+def line_parts(count, chunk, own, wires, sems, emit, follow=None):
     me = lax.axis_index("mp")
     from_low, from_high, to_high, to_low = wires
     up_send, up_recv, down_send, down_recv = sems
@@ -105,26 +86,16 @@
             device_id_type=MESH,
         )
 
-    if greet:
-        greet_line(me, count)
-
-    @pl.when(me == 0)
-    def _():
-        from_low[...] = jnp.zeros_like(from_low)
-
-    @pl.when(me == count - 1)
-    def _():
-        from_high[...] = jnp.zeros_like(from_high)
-
-    def step(at, carry):
-        if prepare is not None and always:
-            prepare(at)
-        elif prepare is not None:
-
-            @pl.when(at < chunks)
-            def _():
-                prepare(at)
-
+    def clear():
+        @pl.when(me == 0)
+        def _():
+            from_low[...] = jnp.zeros_like(from_low)
+
+        @pl.when(me == count - 1)
+        def _():
+            from_high[...] = jnp.zeros_like(from_high)
+
+    def step(at):
         up = at - LINE_LAG * me
 
         @pl.when((up >= 0) & (up < chunks))
@@ -173,22 +144,38 @@
             if follow is not None:
                 follow(ready)
 
+    def drain():
+        def one(index, carry):
+            @pl.when(me < count - 1)
+            def _():
+                up_copy(index).wait_send()
+
+            @pl.when(me > 0)
+            def _():
+                down_copy(index).wait_send()
+
+            return carry
+
+        lax.fori_loop(0, chunks, one, 0)
+
+    return clear, step, drain, chunks + LINE_LAG * (count - 1)
+
+
+def line_sum(count, chunk, own, wires, sems, prepare, emit, follow=None):
+    chunks = own.shape[0] // chunk
+    clear, step, drain, steps = line_parts(count, chunk, own, wires, sems, emit, follow)
+    clear()
+
+    def turn(at, carry):
+        @pl.when(at < chunks)
+        def _():
+            prepare(at)
+
+        step(at)
         return carry
 
-    lax.fori_loop(0, chunks + LINE_LAG * (count - 1), step, 0)
-
-    def drain(index, carry):
-        @pl.when(me < count - 1)
-        def _():
-            up_copy(index).wait_send()
-
-        @pl.when(me > 0)
-        def _():
-            down_copy(index).wait_send()
-
-        return carry
-
-    lax.fori_loop(0, chunks, drain, 0)
+    lax.fori_loop(0, steps, turn, 0)
+    drain()
 
 
 PICK_GROUP = 32
@@ -265,6 +252,7 @@
 LINE_CHUNK = 32
 LINE_LAG = 3
 WORK_ROWS = 256
+FOLLOW_LAG = 28
 
 
 def line_scratch(length, width):
@@ -296,26 +284,67 @@
     )(*operands)
 
 
-def start_kernel(
+def turn_pairs(field, cosine, sine, sign):
+    lane = lax.broadcasted_iota(jnp.int32, field.shape, 1) % HD
+    half = ROT // 2
+    other = jnp.where(
+        lane < half, pltpu.roll(field, field.shape[1] - half, 1), pltpu.roll(field, half, 1)
+    )
+    return field * cosine + sign * other * sine
+
+
+CROSS = (((1,), (1,)), ((), ()))
+
+
+def forward_kernel(
     count,
     part,
     gain,
     shift,
     bias,
     master,
+    cosine,
+    sine,
     w_qkv,
     w_in,
     w_down,
-    rows_out,
+    w_wide,
     attn_out,
-    base_out,
-    ffn_out,
-    pool_out,
+    inner_out,
+    query_out,
+    key_out,
+    value_out,
+    context_out,
+    spread_out,
+    low_out,
+    resid_out,
+    final_out,
+    up_q,
+    up_k,
+    up_v,
+    down_out,
+    up_out,
     *scratch,
 ):
-    (normed, held_qkv, turned, held_in, held_down, sems, pool, near_out, near_in, far_out, far_in) = (
-        scratch[8:]
-    )
+    (
+        own,
+        rows_out,
+        base,
+        ffn,
+        normed,
+        down_qkv,
+        held_qkv,
+        turned,
+        held_in,
+        held_down,
+        w_out,
+        sems,
+        pool,
+        near_out,
+        near_in,
+        far_out,
+        far_in,
+    ) = scratch[16:]
     shards = pool.shape[0]
     splits = shards.bit_length() - 1
     me = lax.axis_index("dp")
@@ -360,17 +389,39 @@
     for offset in range(1, count):
         near(offset).start()
 
-    first, last = 6, part.shape[0] // LINE_CHUNK + 2
+    first, last = 4, FOLLOW_LAG - 6
     waits = (
         [first]
         + [
             first + (last - first) * (2 ** (stage + 1) - 1) // max(1, 2 ** (splits - 1) - 1)
             for stage in range(splits - 1)
         ]
-        + [last + 6]
-    )
-
-    def prepare(at):
+        + [FOLLOW_LAG - 1]
+    )
+
+    own_rows = pool.shape[3]
+    span = count * own_rows
+
+    def strip(shard, matrix):
+        return jnp.concatenate(
+            [pool[shard, m, matrix].astype(jnp.float32) for m in range(count)], 0
+        ).astype(jnp.bfloat16)
+
+    def lay_out():
+        def one(shard, carry):
+            rows = line_chunk(shard, span)
+            for kind in range(3):
+                down_qkv[rows, kind * R : (kind + 1) * R] = strip(shard, kind)
+            up_out[rows, :] = strip(shard, 7)
+            return carry
+
+        lax.fori_loop(0, shards, one, 0)
+        each = shards // count
+        for matrix, ref in ((3, up_q), (4, up_k), (5, up_v), (6, down_out)):
+            for t in range(each):
+                ref[t * span : (t + 1) * span, :] = strip(lane * each + t, matrix)
+
+    def gather_adapters(at):
         for stage in range(splits + 1):
 
             @pl.when(at == waits[stage])
@@ -384,23 +435,25 @@
                 if stage < splits:
                     for copy in far(stage):
                         copy.start()
+                else:
+                    lay_out()
 
     loads = [
         pltpu.make_async_copy(src, dst, sems.at[slot])
         for slot, (src, dst) in enumerate(
-            ((w_qkv, held_qkv), (w_in, held_in), (w_down, held_down))
+            ((w_qkv, held_qkv), (w_in, held_in), (w_down, held_down), (w_wide, w_out))
         )
     ]
     for load in loads:
         load.start()
 
-    def emit(rows, total):
+    def emit_start(rows, total):
         rows_out[rows, :] = total.astype(jnp.bfloat16)
         centre = total - jnp.mean(total, -1, keepdims=True)
         spread = jnp.mean(centre * centre, -1, keepdims=True)
-        base = centre * lax.rsqrt(spread + NORM_EPS)
-        attn_out[rows, :] = (base * gain[0:1, :] + shift[0:1, :]).astype(jnp.bfloat16)
-        normed[rows, :] = (base * gain[1:2, :] + shift[1:2, :]).astype(jnp.bfloat16)
+        flat = centre * lax.rsqrt(spread + NORM_EPS)
+        attn_out[rows, :] = (flat * gain[0:1, :] + shift[0:1, :]).astype(jnp.bfloat16)
+        normed[rows, :] = (flat * gain[1:2, :] + shift[1:2, :]).astype(jnp.bfloat16)
 
     per = WORK_ROWS // LINE_CHUNK
 
@@ -419,7 +472,7 @@
         @pl.when(lax.rem(ready, per) == per - 1)
         def _():
             rows = line_chunk(ready // per, WORK_ROWS)
-            base_out[rows, :] = jnp.dot(
+            base[rows, :] = jnp.dot(
                 attn_out[rows, :], turned[...], preferred_element_type=jnp.float32
             )
             pre = (
@@ -427,71 +480,10 @@
                 + bias[...]
             )
             hidden = (0.5 * pre * (1.0 + lax.erf(pre * 0.5**0.5))).astype(jnp.bfloat16)
-            ffn_out[rows, :] = jnp.dot(
+            ffn[rows, :] = jnp.dot(
                 hidden, held_down[...], preferred_element_type=jnp.float32
             ).astype(jnp.bfloat16)
 
-    line_sum(
-        count,
-        LINE_CHUNK,
-        part,
-        scratch[:4],
-        scratch[4:8],
-        prepare,
-        emit,
-        greet=False,
-        follow=follow,
-        always=True,
-    )
-    pool_out[...] = pool[...]
-    for offset in range(1, count):
-        near(offset).wait_send()
-    for stage in range(splits):
-        for copy in far(stage):
-            copy.wait_send()
-
-
-def turn_pairs(field, cosine, sine, sign):
-    lane = lax.broadcasted_iota(jnp.int32, field.shape, 1) % HD
-    half = ROT // 2
-    other = jnp.where(
-        lane < half, pltpu.roll(field, field.shape[1] - half, 1), pltpu.roll(field, half, 1)
-    )
-    return field * cosine + sign * other * sine
-
-
-CROSS = (((1,), (1,)), ((), ()))
-
-
-def resid_kernel(
-    count,
-    attn,
-    base,
-    ffn,
-    start,
-    gain,
-    shift,
-    cosine,
-    sine,
-    down_qkv,
-    up_q,
-    up_k,
-    up_v,
-    down_out,
-    up_out,
-    w_out,
-    inner_out,
-    query_out,
-    key_out,
-    value_out,
-    context_out,
-    spread_out,
-    low_out,
-    resid_out,
-    final_out,
-    *scratch,
-):
-    own = scratch[8]
     group = w_out.shape[0]
     total_rows = own.shape[0]
     key_out[...] = jnp.zeros_like(key_out)
@@ -500,7 +492,7 @@
     def attend(block):
         rows = line_chunk(block, WORK_ROWS)
         low = jnp.dot(
-            attn[rows, :], down_qkv[...], preferred_element_type=jnp.float32
+            attn_out[rows, :], down_qkv[...], preferred_element_type=jnp.float32
         ).astype(jnp.bfloat16)
         inner_out[rows, :] = low
         for kind, (up, out) in enumerate(
@@ -558,20 +550,42 @@
             + ffn[rows, :].astype(jnp.float32)
         ).astype(jnp.bfloat16)
 
-    per = WORK_ROWS // LINE_CHUNK
-
-    def prepare(at):
-        @pl.when(lax.rem(at, per) == 0)
-        def _():
-            attend(at // per)
-
-    def emit(rows, total):
-        resid = start[rows, :].astype(jnp.float32) + total
+    def emit_resid(rows, total):
+        resid = rows_out[rows, :].astype(jnp.float32) + total
         resid_out[rows, :] = resid
         normed = layer_norm(resid, gain[2:3, :], shift[2:3, :])
         final_out[rows, :] = normed.astype(jnp.bfloat16)
 
-    line_sum(count, LINE_CHUNK, own, scratch[:4], scratch[4:8], prepare, emit)
+    chunks = total_rows // LINE_CHUNK
+    clear, step, drain, steps = line_parts(
+        count, LINE_CHUNK, part, scratch[0:4], scratch[4:8], emit_start, follow
+    )
+    clear_next, step_next, drain_next, steps_next = line_parts(
+        count, LINE_CHUNK, own, scratch[8:12], scratch[12:16], emit_resid
+    )
+    clear()
+    clear_next()
+
+    def turn(at, carry):
+        gather_adapters(at)
+        step(at)
+        later = at - FOLLOW_LAG
+
+        @pl.when((later >= 0) & (later < chunks) & (lax.rem(later, per) == 0))
+        def _():
+            attend(later // per)
+
+        step_next(later)
+        return carry
+
+    lax.fori_loop(0, FOLLOW_LAG + steps_next, turn, 0)
+    drain()
+    drain_next()
+    for offset in range(1, count):
+        near(offset).wait_send()
+    for stage in range(splits):
+        for copy in far(stage):
+            copy.wait_send()
 
 
 DOWN = (((0,), (0,)), ((), ()))
@@ -744,7 +758,6 @@
         scratch[4:8],
         prepare,
         emit,
-        greet=False,
         follow=follow,
     )
     key_grad = jnp.concatenate(
@@ -1132,47 +1145,16 @@
     shards = lax.axis_size("dp")
     own_rows = master.shape[1]
     pool_shape = (shards, group_count, 8, own_rows, R)
-    start_rows, normed_attn, base, ffn_part, pool = line_call(
-        functools.partial(start_kernel, group_count),
-        "start_rows",
-        0,
-        [
-            shape_low,
-            shape_low,
-            jax.ShapeDtypeStruct((rows, w_qkv.shape[1]), jnp.float32),
-            shape_low,
-            jax.ShapeDtypeStruct(pool_shape, jnp.bfloat16),
-        ],
-        line_scratch(rows, D)
-        + [
-            pltpu.VMEM((rows, D), jnp.bfloat16),
-            pltpu.VMEM(w_qkv.shape, jnp.bfloat16),
-            pltpu.VMEM(w_qkv.shape, jnp.bfloat16),
-            pltpu.VMEM(w_in.shape, jnp.bfloat16),
-            pltpu.VMEM(w_down.shape, jnp.bfloat16),
-            pltpu.SemaphoreType.DMA((3,)),
-            pltpu.VMEM(pool_shape, jnp.bfloat16),
-        ]
-        + [pltpu.SemaphoreType.DMA((group_count,))] * 2
-        + [pltpu.SemaphoreType.DMA((shards - 1,))] * 2,
-        [picked, ln_gain, ln_bias, b_in.reshape(1, -1), master, w_qkv, w_in, w_down],
-        spaces=(pl.ANY,) * 3,
-    )
-    adapters = pool.transpose(2, 0, 1, 3, 4).reshape(8, -1, R)
     target = jnp.roll(token_ids, -1, axis=1).reshape(rows)
-    adapter_rows = [
-        lax.dynamic_slice_in_dim(
-            adapters[3 + selector_index], group_index * group_width, group_width, 0
-        )
-        for selector_index in range(3)
-    ]
-    out_rows = lax.dynamic_slice_in_dim(adapters[6], group_index * group_width, group_width, 0)
     cosine, sine = rope_tables(length)
     rest = jnp.zeros((length, HD - ROT), jnp.float32)
     wide_cosine = jnp.concatenate([cosine[:, 0], cosine[:, 0], rest + 1.0] * (128 // HD), 1)
     wide_sine = jnp.concatenate([-sine[:, 0], sine[:, 0], rest] * (128 // HD), 1)
     shape_group = jax.ShapeDtypeStruct((rows, group_width), jnp.bfloat16)
+    low = jnp.bfloat16
+    shape_up = jax.ShapeDtypeStruct((group_width, R), low)
     (
+        normed_attn,
         inner,
         queries,
         key_rows,
@@ -1182,37 +1164,64 @@
         inner_out,
         resid,
         final_rows,
+        up_q,
+        up_k,
+        up_v,
+        down_out,
+        up_out,
     ) = line_call(
-        functools.partial(resid_kernel, group_count),
-        "resid_rows",
-        1,
+        functools.partial(forward_kernel, group_count),
+        "forward",
+        0,
         [
-            jax.ShapeDtypeStruct((rows, 3 * R), jnp.bfloat16),
+            shape_low,
+            jax.ShapeDtypeStruct((rows, 3 * R), low),
             shape_group,
             shape_group,
             shape_group,
             shape_group,
             jax.ShapeDtypeStruct((rows, 128), jnp.float32),
-            jax.ShapeDtypeStruct((rows, R), jnp.bfloat16),
+            jax.ShapeDtypeStruct((rows, R), low),
             shape_wide,
             shape_low,
+            shape_up,
+            shape_up,
+            shape_up,
+            shape_up,
+            jax.ShapeDtypeStruct((D, R), low),
         ],
-        line_scratch(rows, D) + [pltpu.VMEM((rows, D), jnp.bfloat16)],
+        line_scratch(rows, D) * 2
+        + [
+            pltpu.VMEM((rows, D), low),
+            pltpu.VMEM((rows, D), low),
+            pltpu.VMEM((rows, w_qkv.shape[1]), jnp.float32),
+            pltpu.VMEM((rows, D), low),
+            pltpu.VMEM((rows, D), low),
+            pltpu.VMEM((D, 3 * R), low),
+            pltpu.VMEM(w_qkv.shape, low),
+            pltpu.VMEM(w_qkv.shape, low),
+            pltpu.VMEM(w_in.shape, low),
+            pltpu.VMEM(w_down.shape, low),
+            pltpu.VMEM(w_out.shape, low),
+            pltpu.SemaphoreType.DMA((4,)),
+            pltpu.VMEM(pool_shape, low),
+        ]
+        + [pltpu.SemaphoreType.DMA((group_count,))] * 2
+        + [pltpu.SemaphoreType.DMA((shards - 1,))] * 2,
         [
-            normed_attn,
-            base,
-            ffn_part,
-            start_rows,
+            picked,
             ln_gain,
             ln_bias,
+            b_in.reshape(1, -1),
+            master,
             wide_cosine,
             wide_sine,
-            jnp.concatenate([adapters[0], adapters[1], adapters[2]], 1),
-            *adapter_rows,
-            out_rows,
-            adapters[7],
+            w_qkv,
+            w_in,
+            w_down,
             w_out,
         ],
+        spaces=(pl.ANY,) * 4,
     )
     goal = target - group_index * vocab_local
     hits = pick_call(goal, head_rows, "pick_target")
@@ -1228,7 +1237,7 @@
         inner_out,
         normed_attn,
         w_out,
-        adapters[7],
+        up_out,
         wide_cosine,
         wide_sine,
     ]
@@ -1263,8 +1272,10 @@
             hits,
             stats,
             ln_gain,
-            *adapter_rows,
-            out_rows,
+            up_q,
+            up_k,
+            up_v,
+            down_out,
             prompt_len,
             example_len,
             *late,

time: 405 us -> 382 us (0.943)
  Pallas kernels: 365 us -> 348 us
  local copies, waits for them, and re-layouts: 14.4 us -> 9.31 us
    pallas_call x4 -> x3, Pallas kernels: 264 us -> 247 us  [line_call(): pl.pallas_call(kernel, name=name, out_shape=outs, in_specs=[vmem] * (len(...]
  transfers between devices with their start and end apart: 1 -> 1, of which waited for: 0 -> 0; matrix products, arithmetic and copies ran while one was open for 4% -> 3% of each run, Pallas kernels for 40% -> 38%
where the time goes in v2:
time: 382 us
  Pallas kernels  348 us (91%)
  between operations  17.6 us (5%)
  local copies, waits for them, and re-layouts  9.31 us (2%)
  other arithmetic  6.23 us (2%)
    pallas_call x3, Pallas kernels, line_call(): pl.pallas_call(kernel, name=name, out_shape=outs, in_specs=[vmem] * (len(...  247 us
    pallas_call x1, Pallas kernels, loss_call(): pl.pallas_call(functools.partial(loss_kernel, vocab, tile), name='loss',...  71.4 us
    pallas_call x2, Pallas kernels, pick_call(): pl.pallas_call(pick_kernel, name=name, in_specs=[pl.BlockSpec(memory_spac...  29.2 us
  transfers between devices with their start and end apart: 1, of which 0 were waited for; matrix products, arithmetic and copies ran while one was open for 3% of the time, Pallas kernels for 38%

profile of v2, /device:TPU:0, one launch (start us, length us, event | category | flops | bytes accessed | tf_op | source)
XLA Modules:
  0.0 381.8 jit_solution(4811176857259905066)
XLA Ops:
  7.2 0.0 copy-start
  7.2 0.0 all-gather.2.cloned.1.call-start
  7.2 0.7 all-gather.2.cloned.1.call-update
  7.9 0.0 copy-done
  7.9 0.5 slice.9
  8.4 0.1 slice.8
  8.5 0.7 add_subtract_fusion
  9.2 0.2 copy.31
  9.5 0.2 copy.37
  9.7 2.0 fusion.7
  11.7 1.7 concatenate.10.cosine.refs_13_
  13.5 1.8 concatenate.11.sine.refs_14_
  15.3 0.6 fusion.14.spots
  15.9 1.2 fusion.3.places
  17.0 14.6 %pick_start.1.part = bf16[1024,1024]{1,0:T(8,128)(2,1)} custom-call(s32[1024]{0:T(1024)} %fusion.14.spots, s32[1024,1]{1,0:T(8,128)} %fusion.3.places, bf16[12576,1024]{1,0:T(8,128)(2,1)} %table.1), custom_call_target="tpu_custom_call" | custom-call | flops 536870912 | bytes 16777216 | tf_op jit(solution)/shard_map/pick_start/pallas_call | solution.py:229
  31.6 131.8 %forward.1 = (bf16[1024,1024]{1,0:T(8,128)(2,1)}, bf16[1024,384]{1,0:T(8,128)(2,1)}, bf16[1024,256]{1,0:T(8,128)(2,1)}, bf16[1024,256]{1,0:T(8,128)(2,1)}, bf16[...) custom-call(bf16[1024,1024]{1,0:T(8,128)(2,1)} %pick_start.1.part, ...), custom_call_target="tpu_custom_call" | custom-call | bytes 122179840 | tf_op jit(solution)/shard_map/forward/pallas_call | solution.py:270
  163.5 0.6 fusion.16.spots
  164.1 1.1 fusion.6.places
  165.2 0.0 all-gather.2.cloned.1.call-done.table.ahead.behind
  165.2 14.6 %pick_target.1.hits = bf16[1024,1024]{1,0:T(8,128)(2,1)} custom-call(s32[1024]{0:T(1024)} %fusion.16.spots, s32[1024,1]{1,0:T(8,128)} %fusion.6.places, bf16[12576,1024]{1,0:T(8,128)(2,1)} %all-gather.2.cloned.1.call-done.table.ahead.behind), custom_call_target="tpu_custom_call" | custom-call | flops 536870912 | bytes 16777216 | tf_op jit(solution)/shard_map/pick_target/pallas_call | solution.py:229
  179.8 71.4 %loss.1 = (f32[1024,1024]{1,0:T(8,128)}, f32[1024,128]{1,0:T(8,128)}) custom-call(bf16[1024,1024]{1,0:T(8,128)(2,1)} %get-tuple-element.36.values, bf16[12576,1024]{1,0:T(8,128)(2,1)} %all-gather.2.cloned.1.call-done.table.ahead.behind, bf16[12576,1024]{1,0:T(8,128)(2,1)} %all-gather.2.cloned.1.call-done.table.ahead.behind, bf16[1024,1024]{1,0:T(8,128)(2,1)} %pick_target.1.hits), custom_call_target="tpu_custom_call" | custom-call | flops 52747567104 | bytes 51511296 | tf_op jit(solution)/shard_map/loss/pallas_call | solution.py:849
  251.2 78.8 %branch_rows.1 = (f32[1,1024]{1,0:T(1,128)}, f32[1024,128]{1,0:T(8,128)}, f32[1024,128]{1,0:T(8,128)}, f32[1024,128]{1,0:T(8,128)}, f32[1024,128]{1,0:T(8,128)},...) custom-call(f32[1024,1024]{1,0:T(8,128)} %get-tuple-element.37.raw, ...), custom_call_target="tpu_custom_call" | custom-call | bytes 121512256 | tf_op jit(solution)/shard_map/branch_rows/pallas_call | solution.py:270
  330.0 36.7 %fold.1 = (f32[1,1]{1,0:T(1,128)}, f32[1,1]{1,0:T(1,128)}, f32[8,32,128]{2,1,0:T(8,128)}, f32[8,32,128]{2,1,0:T(8,128)}, f32[8,32,128]{2,1,0:T(8,128)}) custom-call(f32[1024,128]{1,0:T(8,128)} %get-tuple-element.53.refs_0_, f32[1024,128]{1,0:T(8,128)} %get-tuple-element.54.refs_1_, f32[1024,128]{1,0:T(8,128)} %get-tuple-element.55.refs_2_, ...), custom_call_target="tpu_custom_call" | custom-call | bytes 103936264 | tf_op jit(solution)/shard_map/fold/pallas_call | solution.py:270
  368.0 1.6 copy.49
  369.5 1.6 copy.50
  371.1 1.6 copy.51
  (3 shorter events, 0.1 us)
Async XLA Ops:
  7.2 0.8 copy-start
  7.2 158.0 %all-gather.2.cloned.1.call-start = ((), (), s32[]{:S(2)}) async-start(), calls=%async_computation | async-start | bytes 28975104 | tf_op jit(solution)/shard_map/all_gather | solution.py:1134
Sparse Core Ops, SparseCore 0:
  9.9 141.1 all-gather.1

commit v3 on v2

--- a/solution.py
+++ b/solution.py
@@ -253,6 +253,7 @@
 LINE_LAG = 3
 WORK_ROWS = 256
 FOLLOW_LAG = 28
+HEAD_STEPS = (33, 48, 64)
 
 
 def line_scratch(length, width):
@@ -262,7 +263,7 @@
     ] * 4
 
 
-def line_call(kernel, name, collective_id, outs, scratch, operands, flops=0, spaces=()):
+def line_call(kernel, name, collective_id, outs, scratch, operands, flops=0, spaces=(), far_outs=0):
     size = sum(o.size * o.dtype.itemsize for o in operands) + sum(
         o.size * o.dtype.itemsize for o in outs
     )
@@ -273,7 +274,8 @@
         out_shape=outs,
         in_specs=[vmem] * (len(operands) - len(spaces))
         + [pl.BlockSpec(memory_space=space) for space in spaces],
-        out_specs=[vmem] * len(outs),
+        out_specs=[vmem] * (len(outs) - far_outs)
+        + [pl.BlockSpec(memory_space=pl.ANY)] * far_outs,
         scratch_shapes=scratch,
         compiler_params=pltpu.CompilerParams(
             collective_id=collective_id, has_side_effects=True, vmem_limit_bytes=VMEM_LIMIT
@@ -297,35 +299,43 @@
 
 
 def forward_kernel(
+    moving,
     count,
     part,
     gain,
     shift,
     bias,
     master,
-    cosine,
-    sine,
+    table,
     w_qkv,
     w_in,
     w_down,
     w_wide,
-    attn_out,
-    inner_out,
-    query_out,
-    key_out,
-    value_out,
-    context_out,
-    spread_out,
-    low_out,
-    resid_out,
-    final_out,
-    up_q,
-    up_k,
-    up_v,
-    down_out,
-    up_out,
-    *scratch,
+    *refs,
 ):
+    head_src = refs[0] if moving else None
+    refs = refs[1:] if moving else refs
+    head_all = refs[17] if moving else None
+    (
+        attn_out,
+        inner_out,
+        query_out,
+        key_out,
+        value_out,
+        context_out,
+        spread_out,
+        low_out,
+        resid_out,
+        final_out,
+        up_q,
+        up_k,
+        up_v,
+        down_out,
+        up_out,
+        cosine_out,
+        sine_out,
+    ) = refs[:17]
+    scratch = refs[18:] if moving else refs[17:]
     (
         own,
         rows_out,
@@ -344,6 +354,7 @@
         near_in,
         far_out,
         far_in,
+        *extra_sems,
     ) = scratch[16:]
     shards = pool.shape[0]
     splits = shards.bit_length() - 1
@@ -389,7 +400,59 @@
     for offset in range(1, count):
         near(offset).start()
 
-    first, last = 4, FOLLOW_LAG - 6
+    def flip(slot, bit):
+        return slot + 2**bit * (1 - 2 * ((slot // 2**bit) % 2))
+
+    def head_copy(half, stage, place):
+        order = ((2, 1, 0), (1, 2, 0))[half]
+        slots = [me]
+        for bit in order[:stage]:
+            slots = slots + [flip(slot, bit) for slot in slots]
+        slot = slots[place]
+        long = head_all.shape[0] // 2
+        rows = pl.ds(half * long, long)
+        wide = head_src.shape[1]
+        there = head_all.at[rows, pl.ds(pl.multiple_of(slot * wide, wide), wide)]
+        index = half * 7 + 2**stage - 1 + place
+        return pltpu.make_async_remote_copy(
+            src_ref=head_src.at[rows] if place == 0 else there,
+            dst_ref=there,
+            send_sem=extra_sems[0].at[index],
+            recv_sem=extra_sems[1].at[index],
+            device_id={"dp": flip(me, order[stage]), "mp": lane},
+            device_id_type=MESH,
+        )
+
+    def head_mine():
+        wide = head_src.shape[1]
+        return pltpu.make_async_copy(
+            head_src,
+            head_all.at[:, pl.ds(pl.multiple_of(me * wide, wide), wide)],
+            extra_sems[2],
+        )
+
+    def head_moves(at):
+        @pl.when(at == HEAD_STEPS[0])
+        def _():
+            for half in range(2):
+                head_copy(half, 0, 0).wait_recv()
+            for half in range(2):
+                head_copy(half, 1, 1).start()
+                head_copy(half, 2, 1).start()
+
+        @pl.when(at == HEAD_STEPS[1])
+        def _():
+            for half in range(2):
+                head_copy(half, 1, 0).wait_recv()
+                head_copy(half, 2, 2).start()
+
+        @pl.when(at == HEAD_STEPS[2])
+        def _():
+            for half in range(2):
+                head_copy(half, 1, 1).wait_recv()
+                head_copy(half, 2, 3).start()
+
+    first, last = 3, 13
     waits = (
         [first]
         + [
@@ -435,6 +498,16 @@
                 if stage < splits:
                     for copy in far(stage):
                         copy.start()
+                    if moving and stage == 0:
+                        head_copy(0, 0, 0).start()
+                        head_copy(1, 1, 0).start()
+                        head_mine().start()
+                    if moving and stage == 1:
+                        head_copy(1, 0, 0).start()
+                        head_copy(0, 1, 0).start()
+                    if moving and stage == 2:
+                        head_copy(0, 2, 0).start()
+                        head_copy(1, 2, 0).start()
                 else:
                     lay_out()
 
@@ -495,6 +568,31 @@
             attn_out[rows, :], down_qkv[...], preferred_element_type=jnp.float32
         ).astype(jnp.bfloat16)
         inner_out[rows, :] = low
+        half = ROT // 2
+        source = lax.broadcasted_iota(jnp.int32, (ROT, 128), 0)
+        into = lax.broadcasted_iota(jnp.int32, (ROT, 128), 1) % HD
+        turning = into < ROT
+        angles = table[rows, :]
+        cosine = jnp.dot(
+            angles,
+            jnp.where(turning & (into % half == source), 1.0, 0.0),
+            precision=HIGH_PRECISION,
+            preferred_element_type=jnp.float32,
+        )
+        lanes = lax.broadcasted_iota(jnp.int32, (WORK_ROWS, 128), 1) % HD
+        cosine = jnp.where(lanes < ROT, cosine, 1.0)
+        sine = jnp.dot(
+            angles,
+            jnp.where(
+                turning & (into % half + half == source),
+                jnp.where(into < half, -1.0, 1.0),
+                0.0,
+            ),
+            precision=HIGH_PRECISION,
+            preferred_element_type=jnp.float32,
+        )
+        cosine_out[rows, :] = cosine
+        sine_out[rows, :] = sine
         for kind, (up, out) in enumerate(
             ((up_q, query_out), (up_k, key_out), (up_v, value_out))
         ):
@@ -508,7 +606,7 @@
                 field = base[rows, kind * group + at : kind * group + at + 128]
                 field = field + extra[:, at : at + 128]
                 if kind < 2:
-                    field = turn_pairs(field, cosine[rows, :], sine[rows, :], 1.0)
+                    field = turn_pairs(field, cosine, sine, 1.0)
                 out[rows, at : at + 128] = field.astype(jnp.bfloat16)
         lane = lax.broadcasted_iota(jnp.int32, (WORK_ROWS, 128), 1)
         column = lax.broadcasted_iota(jnp.int32, (WORK_ROWS, total_rows), 1)
@@ -568,6 +666,8 @@
 
     def turn(at, carry):
         gather_adapters(at)
+        if moving:
+            head_moves(at)
         step(at)
         later = at - FOLLOW_LAG
 
@@ -586,6 +686,15 @@
     for stage in range(splits):
         for copy in far(stage):
             copy.wait_send()
+    if moving:
+        for half in range(2):
+            for place in range(4):
+                head_copy(half, 2, place).wait_recv()
+        head_mine().wait()
+        for half in range(2):
+            for stage in range(splits):
+                for place in range(2**stage):
+                    head_copy(half, stage, place).wait_send()
 
 
 DOWN = (((0,), (0,)), ((), ()))
@@ -1131,10 +1240,13 @@
 ):
     group_count = lax.axis_size("mp")
     group_index = lax.axis_index("mp")
-    head_rows = lax.all_gather(unembed.T, "dp", axis=1, tiled=True)
+    shards = lax.axis_size("dp")
+    moving = shards == 8 and unembed.shape[0] % 128 == 0 and unembed.shape[1] % 32 == 0
+    if not moving:
+        head_rows = lax.all_gather(unembed.T, "dp", axis=1, tiled=True)
     examples, length = token_ids.shape
     width = embedding.shape[0]
-    vocab_local = head_rows.shape[0]
+    vocab_local = unembed.shape[1]
     rows = examples * length
     local_heads = HEADS // group_count
     group_width = local_heads * HD
@@ -1147,9 +1259,7 @@
     pool_shape = (shards, group_count, 8, own_rows, R)
     target = jnp.roll(token_ids, -1, axis=1).reshape(rows)
     cosine, sine = rope_tables(length)
-    rest = jnp.zeros((length, HD - ROT), jnp.float32)
-    wide_cosine = jnp.concatenate([cosine[:, 0], cosine[:, 0], rest + 1.0] * (128 // HD), 1)
-    wide_sine = jnp.concatenate([-sine[:, 0], sine[:, 0], rest] * (128 // HD), 1)
+    table = jnp.concatenate([cosine[:, 0], sine[:, 0]], 1)
     shape_group = jax.ShapeDtypeStruct((rows, group_width), jnp.bfloat16)
     low = jnp.bfloat16
     shape_up = jax.ShapeDtypeStruct((group_width, R), low)
@@ -1169,8 +1279,11 @@
         up_v,
         down_out,
         up_out,
+        wide_cosine,
+        wide_sine,
+        *gathered,
     ) = line_call(
-        functools.partial(forward_kernel, group_count),
+        functools.partial(forward_kernel, moving, group_count),
         "forward",
         0,
         [
@@ -1189,7 +1302,10 @@
             shape_up,
             shape_up,
             jax.ShapeDtypeStruct((D, R), low),
-        ],
+            jax.ShapeDtypeStruct((rows, 128), jnp.float32),
+            jax.ShapeDtypeStruct((rows, 128), jnp.float32),
+        ]
+        + ([jax.ShapeDtypeStruct((vocab_local, D), low)] if moving else []),
         line_scratch(rows, D) * 2
         + [
             pltpu.VMEM((rows, D), low),
@@ -1207,22 +1323,26 @@
             pltpu.VMEM(pool_shape, low),
         ]
         + [pltpu.SemaphoreType.DMA((group_count,))] * 2
-        + [pltpu.SemaphoreType.DMA((shards - 1,))] * 2,
+        + [pltpu.SemaphoreType.DMA((shards - 1,))] * 2
+        + ([pltpu.SemaphoreType.DMA((14,))] * 2 + [pltpu.SemaphoreType.DMA] if moving else []),
         [
             picked,
             ln_gain,
             ln_bias,
             b_in.reshape(1, -1),
             master,
-            wide_cosine,
-            wide_sine,
+            table,
             w_qkv,
             w_in,
             w_down,
             w_out,
-        ],
-        spaces=(pl.ANY,) * 4,
-    )
+        ]
+        + ([unembed.T] if moving else []),
+        spaces=(pl.ANY,) * (5 if moving else 4),
+        far_outs=1 if moving else 0,
+    )
+    if moving:
+        (head_rows,) = gathered
     goal = target - group_index * vocab_local
     hits = pick_call(goal, head_rows, "pick_target")
     raw_grad, stats = loss_call(final_rows, head_rows, hits)

time: 382 us -> 384 us (level)
  Pallas kernels: 348 us -> 366 us
  between operations: 17.6 us -> 4.34 us
    pallas_call x3, Pallas kernels: 247 us -> 266 us  [line_call(): pl.pallas_call(kernel, name=name, out_shape=outs, in_specs=[vmem] * (len(...]
  transfers between devices with their start and end apart: 1 -> 0, of which waited for: 0 -> 0; matrix products, arithmetic and copies ran while one was open for 3% -> 0% of each run, Pallas kernels for 38% -> 0%
where the time goes in v3:
time: 384 us
  Pallas kernels  366 us (95%)
  local copies, waits for them, and re-layouts  8.08 us (2%)
  other arithmetic  5.1 us (1%)
  between operations  4.34 us (1%)
    pallas_call x3, Pallas kernels, line_call(): pl.pallas_call(kernel, name=name, out_shape=outs, in_specs=[vmem] * (len(...  266 us
    pallas_call x1, Pallas kernels, loss_call(): pl.pallas_call(functools.partial(loss_kernel, vocab, tile), name='loss',...  71.4 us
    pallas_call x2, Pallas kernels, pick_call(): pl.pallas_call(pick_kernel, name=name, in_specs=[pl.BlockSpec(memory_spac...  29.2 us

profile of v3, /device:TPU:0, one launch (start us, length us, event | category | flops | bytes accessed | tf_op | source)
XLA Modules:
  0.0 383.9 jit_solution(13425175054401500999)
XLA Ops:
  0.6 1.2 slice.9
  1.8 0.8 slice.8
  2.6 1.4 add_subtract_fusion
  4.0 0.6 fusion.13.spots
  4.6 0.6 fusion.15.spots
  5.2 0.2 fusion.11
  5.4 1.0 copy.36.table
  6.4 0.2 copy.31
  6.7 1.1 fusion.3.places
  7.8 0.2 copy.37
  8.0 1.1 fusion.6.places
  9.1 14.6 %pick_start.1.part = bf16[1024,1024]{1,0:T(8,128)(2,1)} custom-call(s32[1024]{0:T(1024)} %fusion.13.spots, s32[1024,1]{1,0:T(8,128)} %fusion.3.places, bf16[12576,1024]{1,0:T(8,128)(2,1)} %table.1), custom_call_target="tpu_custom_call" | custom-call | flops 536870912 | bytes 16777216 | tf_op jit(solution)/shard_map/pick_start/pallas_call | solution.py:229
  23.7 149.3 %forward.1 = (bf16[1024,1024]{1,0:T(8,128)(2,1)}, bf16[1024,384]{1,0:T(8,128)(2,1)}, bf16[1024,256]{1,0:T(8,128)(2,1)}, bf16[1024,256]{1,0:T(8,128)(2,1)}, bf16[...) custom-call(bf16[1024,1024]{1,0:T(8,128)(2,1)} %pick_start.1.part, ...), custom_call_target="tpu_custom_call" | custom-call | bytes 151220480 | tf_op jit(solution)/shard_map/forward/pallas_call | solution.py:271
  173.0 14.6 %pick_target.1.hits = bf16[1024,1024]{1,0:T(8,128)(2,1)} custom-call(s32[1024]{0:T(1024)} %fusion.15.spots, s32[1024,1]{1,0:T(8,128)} %fusion.6.places, bf16[12576,1024]{1,0:T(8,128)(2,1)} %get-tuple-element.40.table.ahead.behind), custom_call_target="tpu_custom_call" | custom-call | flops 536870912 | bytes 16777216 | tf_op jit(solution)/shard_map/pick_target/pallas_call | solution.py:229
  187.6 71.4 %loss.1 = (f32[1024,1024]{1,0:T(8,128)}, f32[1024,128]{1,0:T(8,128)}) custom-call(bf16[1024,1024]{1,0:T(8,128)(2,1)} %get-tuple-element.39.values, bf16[12576,1024]{1,0:T(8,128)(2,1)} %get-tuple-element.40.table.ahead.behind, bf16[12576,1024]{1,0:T(8,128)(2,1)} %get-tuple-element.40.table.ahead.behind, bf16[1024,1024]{1,0:T(8,128)(2,1)} %pick_target.1.hits), custom_call_target="tpu_custom_call" | custom-call | flops 52747567104 | bytes 51511296 | tf_op jit(solution)/shard_map/loss/pallas_call | solution.py:958
  259.0 80.2 %branch_rows.1 = (f32[1,1024]{1,0:T(1,128)}, f32[1024,128]{1,0:T(8,128)}, f32[1024,128]{1,0:T(8,128)}, f32[1024,128]{1,0:T(8,128)}, f32[1024,128]{1,0:T(8,128)},...) custom-call(f32[1024,1024]{1,0:T(8,128)} %get-tuple-element.41.raw, ...), custom_call_target="tpu_custom_call" | custom-call | bytes 121512256 | tf_op jit(solution)/shard_map/branch_rows/pallas_call | solution.py:271
  339.2 36.3 %fold.1 = (f32[1,1]{1,0:T(1,128)}, f32[1,1]{1,0:T(1,128)}, f32[8,32,128]{2,1,0:T(8,128)}, f32[8,32,128]{2,1,0:T(8,128)}, f32[8,32,128]{2,1,0:T(8,128)}) custom-call(f32[1024,128]{1,0:T(8,128)} %get-tuple-element.59.refs_0_, f32[1024,128]{1,0:T(8,128)} %get-tuple-element.60.refs_1_, f32[1024,128]{1,0:T(8,128)} %get-tuple-element.61.refs_2_, ...), custom_call_target="tpu_custom_call" | custom-call | bytes 103936264 | tf_op jit(solution)/shard_map/fold/pallas_call | solution.py:271
  376.9 1.6 copy.49
  378.5 1.6 copy.50
  380.1 1.6 copy.51
  (2 shorter events, 0.0 us)
